TPU v7x, 256 devices: a whole 4x4x8 slice. The times are simulated.
256 devices in a mesh: dp: 8 (over z), expert: 32 (over y, x, core).
Axes of the slice: x: 4, y: 4, z: 8, core: 2. Of those that a mesh axis runs over, the one named last changes fastest.
Arguments:
- hidden_in: bfloat16 [1024, 5120], P(('dp', 'expert')), may hold values from -6 to 6
- query: bfloat16 [1024, 36864], P(('dp', 'expert')), may hold values from -6 to 24
- prefix_pool: bfloat16 [128, 36864], P('dp'), may hold values from -6 to 6
- suffix_cache: bfloat16 [1024, 73728], P(('dp', 'expert')), may hold values from -6 to 6
- block_list: int32 [1024, 32], P(('dp', 'expert')), may hold values from 0 to 127, as said below
- prefix_count: int32 [1024], P(('dp', 'expert')), may hold values from 1 to 32
- suffix_count: int32 [1024], P(('dp', 'expert')), may hold values from 1 to 128
- value_up: bfloat16 [64, 512, 128], P('expert'), may hold values from -0.25 to 0.25
- out_proj: bfloat16 [8192, 5120], P('expert'), may hold values from -0.5 to 0.5
- norm_gain: bfloat16 [5120], replicated, may hold values from 0.5 to 1.5
- expert_ids: int32 [1024, 6], P(('dp', 'expert')), may hold values from 0 to 31, all different within a row; in each aligned block of 4 rows (0 to 3, 4 to 7, ...) at most 2 rows name the same one
- gate_weights: bfloat16 [1024, 6], P(('dp', 'expert')), may hold values from 0.049804688 to 1
- gate_proj: bfloat16 [32, 5120, 1536], P('expert', None, 'dp'), may hold values from -0.078125 to 0.078125
- up_proj: bfloat16 [32, 5120, 1536], P('expert', None, 'dp'), may hold values from -0.078125 to 0.078125
- down_proj: bfloat16 [32, 1536, 5120], P('expert', 'dp'), may hold values from -0.15625 to 0.15625
Outputs:
- residual_out: float32 [1024, 5120], P(('dp', 'expert'))
- moe_out: float32 [1024, 5120], P(('dp', 'expert'))
Inputs may be any that keep to these rules, and one draw needn't show every extreme that they name: `block_list`: each list names 32 distinct blocks; the lists form a prefix tree: two requests with the same block at a position have the same blocks at all earlier positions. `expert_ids`: each row names 6 different experts; among the rows of one device no expert is named more than 2 times.
All inputs are finite; a program needn't handle non-finite values.
Results may differ from a plain program's by a relative error of at most 0.025.
Values may be sent and summed in bfloat16 or wider, within the bound.
A program may use at most 128 MiB of HBM per device.

v0:
```python
import jax
import jax.numpy as jnp
from jax import lax
from jax.sharding import PartitionSpec as P

HEADS = 64
LAT = 512
TOPK = 6
BLOCK = 64
SUFFIX = 128
KDIM = 576


NEG_FILL = -1e30
SCORE_SCALE = 192.0 ** (-0.5)
NORM_EPS = 1e-06


def slot_table(expert_rows, expert_total):
    matches = (expert_rows[..., None] == jnp.arange(expert_total, dtype=jnp.int32)).astype(
        jnp.int32
    )
    row_load = jnp.sum(matches, axis=-2)
    earlier = jnp.cumsum(row_load, axis=-2) - row_load
    return jnp.sum(matches * earlier[..., None, :], axis=-1)


def dispatch_matrix(expert_rows, slot_rows, expert_total, capacity):
    expert_match = expert_rows[..., None] == jnp.arange(expert_total, dtype=jnp.int32)
    slot_match = slot_rows[..., None] == jnp.arange(capacity, dtype=jnp.int32)
    joined = expert_match[..., :, None] & slot_match[..., None, :]
    return jnp.any(joined, axis=-3).astype(jnp.bfloat16)


def merge_keys(state, queries, key_rows, live_mask):
    running_max, running_sum, numerator = state
    scores = (
        jnp.einsum("rhk,nk->rhn", queries, key_rows, preferred_element_type=jnp.float32)
        * SCORE_SCALE
    )
    live_keys = live_mask[:, None, :]
    scores = jnp.where(live_keys, scores, NEG_FILL)
    new_max = jnp.maximum(running_max, jnp.max(scores, axis=-1))
    weights = jnp.where(live_keys, jnp.exp(scores - new_max[..., None]), 0.0)
    rescale = jnp.exp(running_max - new_max)
    running_sum = running_sum * rescale + jnp.sum(weights, axis=-1)
    numerator = numerator * rescale[..., None] + jnp.einsum(
        "rhn,nl->rhl",
        weights.astype(jnp.bfloat16),
        key_rows[:, :LAT],
        preferred_element_type=jnp.float32,
    )
    return (new_max, running_sum, numerator)


def prefix_partial(state, pool_piece, queries, block_rows, counts):
    piece_blocks = pool_piece.shape[0]
    key_rows = pool_piece.reshape(piece_blocks * BLOCK, KDIM)
    block_ids = jnp.arange(piece_blocks, dtype=jnp.int32)
    in_prefix = jnp.arange(block_rows.shape[1], dtype=jnp.int32)[None, :] < counts[:, None]
    member = jnp.any(
        (block_rows[:, :, None] == block_ids[None, None, :]) & in_prefix[:, :, None], axis=1
    )
    live_mask = jnp.repeat(member, BLOCK, axis=1)
    return merge_keys(state, queries, key_rows, live_mask)


def own_partial(queries, own_keys, own_live):
    scores = (
        jnp.einsum("rhk,rnk->rhn", queries, own_keys, preferred_element_type=jnp.float32)
        * SCORE_SCALE
    )
    live_keys = own_live[:, None, :]
    scores = jnp.where(live_keys, scores, NEG_FILL)
    row_max = jnp.max(scores, axis=-1)
    weights = jnp.where(live_keys, jnp.exp(scores - row_max[..., None]), 0.0)
    numerator = jnp.einsum(
        "rhn,rnl->rhl",
        weights.astype(jnp.bfloat16),
        own_keys[:, :, :LAT],
        preferred_element_type=jnp.float32,
    )
    return (row_max, jnp.sum(weights, axis=-1), numerator)


def run_experts(arrived, expert_axis, gate_proj, up_proj, down_proj):
    local_count = gate_proj.shape[0]
    arrived_shape = arrived.shape
    grouped = arrived.reshape(
        arrived_shape[:expert_axis]
        + (arrived_shape[expert_axis] // local_count, local_count)
        + arrived_shape[expert_axis + 1 :]
    )
    selected = lax.index_in_dim(grouped, 0, expert_axis + 1, keepdims=False)
    flat_rows = selected.reshape(-1, arrived_shape[-1])
    gate_part = jnp.dot(flat_rows, gate_proj[0], preferred_element_type=jnp.float32)
    up_part = jnp.dot(flat_rows, up_proj[0], preferred_element_type=jnp.float32)
    hidden = (jax.nn.silu(gate_part) * up_part).astype(jnp.bfloat16)
    result = jnp.dot(hidden, down_proj[0], preferred_element_type=jnp.float32).astype(jnp.bfloat16)
    outputs = [result.reshape(selected.shape)]
    return jnp.stack(outputs, axis=expert_axis + 1).reshape(arrived_shape)


def per_device(
    hidden_in,
    query,
    prefix_pool,
    suffix_cache,
    block_list,
    prefix_count,
    suffix_count,
    value_up,
    out_proj,
    norm_gain,
    expert_ids,
    gate_weights,
    gate_proj,
    up_proj,
    down_proj,
):
    row_count = hidden_in.shape[0]
    queries = query.reshape(row_count, HEADS, KDIM)
    own_keys = suffix_cache.reshape(row_count, SUFFIX, KDIM)
    own_live = jnp.arange(SUFFIX, dtype=jnp.int32)[None, :] < suffix_count[:, None]
    own_state = own_partial(queries, own_keys, own_live)
    running_max, running_sum, numerator = prefix_partial(
        own_state,
        lax.all_gather(prefix_pool, "dp", axis=0, tiled=True),
        queries,
        block_list,
        prefix_count,
    )
    context = (numerator / running_sum[..., None]).astype(jnp.bfloat16)
    head_context = lax.all_to_all(context, "expert", split_axis=1, concat_axis=0, tiled=True)
    head_values = jnp.einsum(
        "thl,hlv->thv", head_context, value_up, preferred_element_type=jnp.float32
    ).astype(jnp.bfloat16)
    value_rows = head_values.reshape(head_values.shape[0], -1)
    attended = lax.psum_scatter(
        jnp.dot(value_rows, out_proj, preferred_element_type=jnp.float32),
        "expert",
        scatter_dimension=0,
        tiled=True,
    )
    residual_out = hidden_in.astype(jnp.float32) + attended
    scale_rows = lax.rsqrt(jnp.mean(residual_out * residual_out, axis=-1, keepdims=True) + NORM_EPS)
    normed = (residual_out * scale_rows * norm_gain.astype(jnp.float32)).astype(jnp.bfloat16)
    expert_total = gate_proj.shape[0] * lax.axis_size("expert")
    capacity = max(2, (row_count * TOPK + expert_total - 1) // expert_total)
    group_tokens, group_ids, group_gates = (
        lax.all_gather(normed, "dp", axis=0, tiled=True),
        lax.all_gather(expert_ids, "dp", axis=0, tiled=True),
        lax.all_gather(gate_weights, "dp", axis=0, tiled=True),
    )
    holders = lax.axis_size("dp")
    group_tokens = group_tokens.reshape(holders, row_count, -1)
    group_ids = group_ids.reshape(holders, row_count, TOPK)
    group_gates = group_gates.reshape(holders, row_count, TOPK).astype(jnp.float32)
    group_slots = slot_table(group_ids, expert_total)
    dispatch_table = dispatch_matrix(group_ids, group_slots, expert_total, capacity)
    outgoing = jnp.einsum(
        "nrec,nrd->encd", dispatch_table, group_tokens, preferred_element_type=jnp.float32
    ).astype(jnp.bfloat16)
    finished = run_experts(
        lax.all_to_all(outgoing, "expert", split_axis=0, concat_axis=0, tiled=True),
        0,
        gate_proj,
        up_proj,
        down_proj,
    )
    returned = lax.all_to_all(finished, "expert", split_axis=0, concat_axis=0, tiled=True)
    source_rows = jnp.arange(holders, dtype=jnp.int32)[:, None, None]
    picked = returned[group_ids, source_rows, group_slots]
    weighted = jnp.sum(picked.astype(jnp.float32) * group_gates[..., None], axis=2)
    moe_sum = lax.psum_scatter(weighted, "dp", scatter_dimension=0, tiled=True).reshape(
        row_count, -1
    )
    return (residual_out, moe_sum)


def solution(mesh):
    in_specs = (
        P(("dp", "expert"), None),
        P(("dp", "expert"), None),
        P("dp", None),
        P(("dp", "expert"), None),
        P(("dp", "expert"), None),
        P(("dp", "expert")),
        P(("dp", "expert")),
        P("expert", None, None),
        P("expert", None),
        P(),
        P(("dp", "expert"), None),
        P(("dp", "expert"), None),
        P("expert", None, "dp"),
        P("expert", None, "dp"),
        P("expert", "dp", None),
    )
    out_specs = (P(("dp", "expert"), None), P(("dp", "expert"), None))
    return jax.shard_map(
        per_device, mesh=mesh, in_specs=in_specs, out_specs=out_specs, check_vma=False
    )
```

profile of v0, /device:TPU:2, one launch (start us, length us, event | category | flops | bytes accessed | tf_op | source)
XLA Modules:
  0.0 604.3 jit_solution(14038184007065560886)
XLA Ops:
  15.9 100.8 %all-gather.5.cloned.1.call-done = bf16[128,36864]{1,0:T(8,128)(2,1)} async-done(((bf16[16,36864]{1,0:T(8,128)(2,1)}), bf16[128,36864]{1,0:T(8,128)(2,1)}) %all-gather.5.cloned.1.call-update) | async-done | bytes 9437200 | tf_op jit(solution)/shard_map/all_gather | solution.py:128
  116.8 18.4 %reshape.167 = bf16[8192,576]{1,0:T(8,128)(2,1)} reshape(bf16[128,36864]{1,0:T(8,128)(2,1)} %all-gather.5.cloned.1.call-done) | data formatting | bytes 18874368 | tf_op jit(solution)/shard_map/reshape | solution.py:58
  135.2 11.3 %fusion.57 = (f32[4,64]{1,0:T(4,128)S(1)}, f32[4,64,8192]{2,1,0:T(8,128)}) fusion(bf16[4,64,576]{2,1,0:T(8,128)(2,1)} %reshape.165, bf16[8192,576]{1,0:T(8,128)(2,1)} %reshape.167, pred[4,8192]{1,0:T(4,128)(4,1)S(1)} %broadcast_in_dim.75), kind=kOutput, calls=%fused_computation.77 | convolution fusion | flops 2422210304 | bytes 18154496 | tf_op jit(solution)/shard_map/rhk,nk->rhn/dot_general | solution.py:38
  146.5 5.9 fusion.4
  154.9 14.9 %all_to_all.28 = bf16[4,64,512]{2,0,1:T(4,128)(2,1)S(1)} all-to-all(bf16[4,64,512]{2,0,1:T(4,128)(2,1)S(1)} %copy.34), channel_id=1, replica_groups=mesh['dp'=8,'expert'=32] {'expert'}, dimensions={1} | all-to-all | bytes 524288 | tf_op jit(solution)/shard_map/all_to_all | solution.py:134
  171.2 2.1 fusion.58
  173.3 21.4 %all-gather.1 = s32[8,4,6]{2,1,0:T(4,128)S(1)} all-gather(s32[1,4,6]{2,1,0:T(4,128)S(1)} %bitcast.68), channel_id=1, replica_groups=mesh['dp'=8,'expert'=32] {'dp'}, dimensions={0}, use_global_device_ids=true | all-gather | bytes 864 | tf_op jit(solution)/shard_map/all_gather | solution.py:152
  197.1 90.6 %all-reduce.5.cloned.1.call-done = f32[128,5120]{1,0:T(8,128)} async-done(((f32[128,5120]{1,0:T(8,128)}), f32[128,5120]{1,0:T(8,128)}) %all-reduce.5.cloned.1.call-update) | async-done | bytes 2621456
  288.9 26.6 %all-gather = bf16[8,4,5120]{2,1,0:T(4,128)(2,1)S(1)} all-gather(bf16[1,4,5120]{2,1,0:T(4,128)(2,1)S(1)} %fusion.45), channel_id=1, replica_groups=mesh['dp'=8,'expert'=32] {'dp'}, dimensions={0}, use_global_device_ids=true | all-gather | bytes 368640 | tf_op jit(solution)/shard_map/all_gather | solution.py:151
  315.5 3.9 fusion.7
  319.4 10.2 %copy.39 = bf16[32,8,2,5120]{3,2,1,0:T(2,128)(2,1)} copy(bf16[32,8,2,5120]{3,0,2,1:T(8,128)(2,1)} %fusion.7) | data formatting | bytes 10485760 | tf_op jit(solution)/shard_map/convert_element_type | solution.py:163
  329.6 67.3 %all_to_all.29 = bf16[32,8,2,5120]{3,2,1,0:T(2,128)(2,1)} all-to-all(bf16[32,8,2,5120]{3,2,1,0:T(2,128)(2,1)} %copy.39), channel_id=1, replica_groups=mesh['dp'=8,'expert'=32] {'expert'}, dimensions={0} | all-to-all | bytes 10485760 | tf_op jit(solution)/shard_map/all_to_all | solution.py:165
  396.9 11.5 %reshape_squeeze_reshape.3 = bf16[512,5120]{1,0:T(8,128)(2,1)} reshape(bf16[32,8,2,5120]{3,2,1,0:T(2,128)(2,1)} %all_to_all.29) | data formatting | bytes 10485760 | tf_op jit(solution)/shard_map/reshape;squeeze;reshape | solution.py:95
  408.4 4.3 fusion.15
  412.7 9.4 %convolution_convert_fusion = bf16[512,5120]{1,0:T(8,128)(2,1)} fusion(bf16[1,192,5120]{2,1,0:T(8,128)(2,1)} %param.29, bf16[512,5120]{1,0:T(8,128)(2,1)} %reshape_squeeze_reshape.3, bf16[1,5120,192]{1,2,0:T(8,128)(2,1)} %param.28, f32[512,192]{0,1:T(8,128)S(1)} %fusion.15), kind=kOutput, calls=%fused_computation.7 | convolution fusion | flops 2016477184 | bytes 14811136 | tf_op jit(solution)/shard_map/dot_general | solution.py:99
  422.2 11.0 %reshape_stack_reshape.3 = bf16[32,8,2,5120]{3,2,1,0:T(2,128)(2,1)} reshape(bf16[512,5120]{1,0:T(8,128)(2,1)} %convolution_convert_fusion) | data formatting | bytes 10485760 | tf_op jit(solution)/shard_map/reshape;stack;reshape | solution.py:101
  433.2 6.1 %all-to-all-start.2 = ((bf16[32,8,2,5120]{3,2,1,0:T(2,128)(2,1)}), bf16[32,8,2,5120]{3,2,1,0:T(2,128)(2,1)}, u32[]{:S(2)}, u32[]{:S(2)}) async-start(bf16[32,8,2,5120]{3,2,1,0:T(2,128)(2,1)} %reshape_stack_reshape.3), calls=%async_computation.2 | async-start | bytes 10485760 | tf_op jit(solution)/shard_map/all_to_all | solution.py:171
  439.5 15.4 %all-gather.2 = bf16[8,4,6]{2,1,0:T(4,128)(2,1)S(1)} all-gather(bf16[1,4,6]{2,1,0:T(4,128)(2,1)S(1)} %bitcast.69), channel_id=1, replica_groups=mesh['dp'=8,'expert'=32] {'dp'}, dimensions={0}, use_global_device_ids=true | all-gather | bytes 432 | tf_op jit(solution)/shard_map/all_gather | solution.py:153
  455.0 47.5 %all-to-all-done.2 = bf16[32,8,2,5120]{3,2,1,0:T(2,128)(2,1)} async-done(((bf16[32,8,2,5120]{3,2,1,0:T(2,128)(2,1)}), bf16[32,8,2,5120]{3,2,1,0:T(2,128)(2,1)}, u32[]{:S(2)}, u32[]{:S(2)}) %all-to-all-start.2) | async-done | bytes 5242912 | tf_op jit(solution)/shard_map/all_to_all | solution.py:171
  502.5 10.7 %gather_fusion = bf16[192,5120]{1,0:T(8,128)(2,1)} fusion(bf16[32,8,2,5120]{3,2,1,0:T(2,128)(2,1)} %all-to-all-done.2, s32[192]{0:T(256)S(1)} %reshape.173), kind=kCustom, calls=%fused_computation | custom fusion | bytes 3934464 | tf_op jit(solution)/shard_map/gather | solution.py:173
  513.2 4.5 reshape.179
  517.7 5.3 multiply_reduce_fusion
  523.6 71.6 %all-reduce.7.cloned.1.call-done = f32[8,4,5120]{2,1,0:T(4,128)} async-done(((f32[8,4,5120]{2,1,0:T(4,128)}), f32[8,4,5120]{2,1,0:T(4,128)}) %all-reduce.7.cloned.1.call-update) | async-done | bytes 655376
  595.2 2.1 dynamic-slice_bitcast_fusion
  (64 shorter events, 16.3 us)
Async XLA Ops:
  7.2 164.0 %copy-start = (bf16[256,5120]{1,0:T(8,128)(2,1)S(1)}, bf16[256,5120]{1,0:T(8,128)(2,1)}, u32[]{:S(2)}) copy-start(bf16[256,5120]{1,0:T(8,128)(2,1)} %param.23) | copy-start | bytes 7864324
  7.2 109.6 %all-gather.5.cloned.1.call-start = ((), (), s32[]{:S(2)}) async-start(), calls=%async_computation.3 | async-start | bytes 10616832 | tf_op jit(solution)/shard_map/all_gather | solution.py:128
  7.9 279.8 %all-reduce.5.cloned.1.call-start = ((), (), s32[]{:S(2)}) async-start(), calls=%async_computation.4 | async-start | bytes 5242880
  135.2 11.3 %copy-start.2 = (bf16[8192,576]{1,0:T(8,128)(2,1)S(1)}, bf16[8192,576]{1,0:T(8,128)(2,1)}, u32[]{:S(2)}) copy-start(bf16[8192,576]{1,0:T(8,128)(2,1)} %reshape.167) | copy-start | bytes 28311556
  146.5 5.9 copy-start.3
  154.6 18.7 %copy-start.6 = (bf16[5120]{0:T(1024)(128)(2,1)S(1)}, bf16[5120]{0:T(1024)(128)(2,1)}, u32[]{:S(2)}) copy-start(bf16[5120]{0:T(1024)(128)(2,1)} %param.24) | copy-start | bytes 30724
  154.6 18.7 %copy-start.7 = (s32[4,6]{1,0:T(4,128)S(1)}, s32[4,6]{1,0:T(4,128)}, u32[]{:S(2)}) copy-start(s32[4,6]{1,0:T(4,128)} %param.25) | copy-start | bytes 292
  154.6 40.2 %copy-start.11 = (u32[256]{0:T(256)S(1)}, u32[256]{0:T(256)}, u32[]{:S(2)}) copy-start(u32[256]{0:T(256)} %constant.66) | copy-start | bytes 3076
  154.9 132.9 %copy-start.5 = (bf16[4,5120]{1,0:T(4,128)(2,1)S(1)}, bf16[4,5120]{1,0:T(4,128)(2,1)}, u32[]{:S(2)}) copy-start(bf16[4,5120]{1,0:T(4,128)(2,1)} %param.15) | copy-start | bytes 122884
  288.8 40.8 %copy-start.4 = (f32[4,5120]{1,0:T(4,128)}, f32[4,5120]{1,0:T(4,128)S(1)}, u32[]{:S(2)}) copy-start(f32[4,5120]{1,0:T(4,128)S(1)} %get-tuple-element.3) | copy-start | bytes 245764
  396.9 11.5 %copy-start.9 = (bf16[1,5120,192]{1,2,0:T(8,128)(2,1)S(1)}, bf16[1,5120,192]{1,2,0:T(8,128)(2,1)}, u32[]{:S(2)}) copy-start(bf16[1,5120,192]{1,2,0:T(8,128)(2,1)} %param.27) | copy-start | bytes 5898244
  433.2 6.4 %copy-start.8 = (bf16[4,6]{1,0:T(4,128)(2,1)S(1)}, bf16[4,6]{1,0:T(4,128)(2,1)}, u32[]{:S(2)}) copy-start(bf16[4,6]{1,0:T(4,128)(2,1)} %param.26) | copy-start | bytes 148
  433.2 69.4 %all-to-all-start.2 = ((bf16[32,8,2,5120]{3,2,1,0:T(2,128)(2,1)}), bf16[32,8,2,5120]{3,2,1,0:T(2,128)(2,1)}, u32[]{:S(2)}, u32[]{:S(2)}) async-start(bf16[32,8,2,5120]{3,2,1,0:T(2,128)(2,1)} %reshape_stack_reshape.3), calls=%async_computation.2 | async-start | bytes 10485760 | tf_op jit(solution)/shard_map/all_to_all | solution.py:171
  439.2 156.0 %all-reduce.7.cloned.1.call-start = ((), (), s32[]{:S(2)}) async-start(), calls=%async_computation.5 | async-start | bytes 1310720
  502.5 94.8 %copy-start.1 = (bf16[256,5120]{1,0:T(8,128)(2,1)S(1)}, bf16[256,5120]{1,0:T(8,128)(2,1)}, u32[]{:S(2)}) copy-start(bf16[256,5120]{1,0:T(8,128)(2,1)} %param.23) | copy-start | bytes 7864324
  513.2 9.8 %copy-start.10 = (u32[256]{0:T(256)S(1)}, u32[256]{0:T(256)}, u32[]{:S(2)}) copy-start(u32[256]{0:T(256)} %constant.70) | copy-start | bytes 3076
Sparse Core Ops, SparseCore 0:
  9.8 106.9 all-gather.4
  173.4 114.3 all-reduce.4
  523.2 71.9 all-reduce.6
where the time goes:
time: 614 us; the launch traced here: 604 us
  waiting for transfers between devices  311 us (51%)
  blocking collectives  146 us (24%)
  local copies, waits for them, and re-layouts  74.5 us (12%)
  matrix products  39.9 us (6%)
  between operations  15.1 us (2%)
  other arithmetic  11.8 us (2%)
  starting transfers between devices  6.19 us (1%)
    unnamed x5, waiting for transfers between devices  163 us
    all_gather x1, waiting for transfers between devices, per_device(): lax.all_gather(prefix_pool, 'dp', axis=0, tiled=True)  101 us
    all_to_all x1, blocking collectives, per_device(): lax.all_to_all(outgoing, 'expert', split_axis=0, concat_axis=0, tiled=True)  67.3 us
    all_to_all x1, waiting for transfers between devices, per_device(): lax.all_to_all(finished, 'expert', split_axis=0, concat_axis=0, tiled=True)  47.5 us
    all_gather x1, blocking collectives, per_device(): lax.all_gather(normed, 'dp', axis=0, tiled=True)  26.6 us
    all_gather x1, blocking collectives, per_device(): lax.all_gather(expert_ids, 'dp', axis=0, tiled=True)  21.4 us
    reshape x1, local copies, waits for them, and re-layouts, prefix_partial(): key_rows = pool_piece.reshape(piece_blocks * BLOCK, KDIM)  18.4 us
    all_gather x1, blocking collectives, per_device(): lax.all_gather(gate_weights, 'dp', axis=0, tiled=True)  15.4 us
  transfers between devices with their start and end apart: 4, of which 4 were waited for; matrix products, arithmetic and copies ran while one was open for 2% of the time, Pallas kernels for 0%

commit v1 on v0

v1 whole, which is shorter than its diff:
```python
import functools
import jax
import jax.numpy as jnp
from jax import lax
from jax.experimental import pallas as pl
from jax.experimental.pallas import tpu as pltpu
from jax.sharding import PartitionSpec as P

HEADS = 64
LAT = 512
BLOCK = 64
SUFFIX = 128
KDIM = 576
KPAD = 640
D = 5120
HALF = 2560
FFG = 192
TABLE = 128

NEG_FILL = -1e30
SCORE_SCALE = 192.0 ** (-0.5)
NORM_EPS = 1e-06

NX, NY, NZ = 4, 4, 8
MESH = pl.DeviceIdType.MESH
F32 = jnp.float32
BF16 = jnp.bfloat16


def here():
    z = lax.axis_index("dp")
    e = lax.axis_index("expert")
    core = lax.rem(e, 2)
    chip = lax.div(e, 2)
    return z, lax.div(chip, NX), lax.rem(chip, NX), core


def dev(z, y, x, core):
    return (z, (y * NX + x) * 2 + core)


def step(v, by, n):
    return lax.rem(v + by + n, n)


def greet(peers):
    barrier = pltpu.get_barrier_semaphore()
    for peer in peers:
        pl.semaphore_signal(barrier, inc=1, device_id=peer, device_id_type=MESH)
    pl.semaphore_wait(barrier, len(peers))


def torus_peers(z, y, x, c):
    peers = [dev(step(z, j, NZ), y, x, c) for j in range(1, NZ)]
    peers += [dev(z, y, step(x, s, NX), c) for s in (1, -1)]
    peers += [dev(z, step(y, s, NY), x, c) for s in (1, -1)]
    return peers + [dev(z, y, x, 1 - c)]


class Post:
    def __init__(self, send, recv):
        self.send, self.recv, self.count, self.sent = send, recv, 0, []

    def put(self, src, dst, to, lands):
        i = self.count
        self.count += 1
        copy = pltpu.make_async_remote_copy(
            src_ref=src, dst_ref=dst, send_sem=self.send.at[i], recv_sem=self.recv.at[i],
            device_id=to, device_id_type=MESH,
        )
        copy.start()
        self.sent.append(copy)
        return pltpu.make_async_remote_copy(
            src_ref=lands, dst_ref=lands, send_sem=self.send.at[i], recv_sem=self.recv.at[i],
            device_id=to, device_id_type=MESH,
        ).wait_recv

    def drain(self):
        for copy in self.sent:
            copy.wait_send()


def gather(post, block, g, rows, local_sem):
    z, y, x, c = here()
    xp, xm, x2 = step(x, 1, NX), step(x, -1, NX), step(x, 2, NX)
    yp, ym, y2 = step(y, 1, NY), step(y, -1, NY), step(y, 2, NY)
    quarter = 2 * rows
    a_lo, a_hi, a_all = pl.ds(0, quarter), pl.ds(quarter, quarter), pl.ds(0, 2 * quarter)
    b_lo, b_hi, b_all = (
        pl.ds(2 * quarter, quarter), pl.ds(3 * quarter, quarter), pl.ds(2 * quarter, 2 * quarter)
    )

    def zrows(at):
        return pl.ds(pl.multiple_of(at * rows, rows), rows)

    def slot(yy, xx, part):
        return g.at[c, yy, xx, part]

    keep = pltpu.make_async_copy(block, slot(y, x, zrows(z)), local_sem)
    keep.start()
    arrive = [
        post.put(block, slot(y, x, zrows(z)), dev(step(z, j, NZ), y, x, c), slot(y, x, zrows(step(z, -j, NZ))))
        for j in range(1, NZ)
    ]
    yield []
    keep.wait()
    for wait in arrive:
        wait()

    from_sibling = {}

    def sibling(name, yy, xx, part):
        from_sibling[name] = post.put(
            slot(yy, xx, part), slot(yy, xx, part), dev(z, y, x, 1 - c), g.at[1 - c, yy, xx, part]
        )

    def along_x(yy, xx, part, by):
        return post.put(
            slot(yy, xx, part), slot(yy, xx, part), dev(z, y, step(x, by, NX), c),
            slot(yy, step(xx, -by, NX), part),
        )

    def along_y(yy, xx, part, by):
        return post.put(
            slot(yy, xx, part), slot(yy, xx, part), dev(z, step(y, by, NY), x, c),
            slot(step(yy, -by, NY), xx, part),
        )

    a1p, a1m = along_x(y, x, a_all, 1), along_x(y, x, a_all, -1)
    b1p, b1m = along_y(y, x, b_all, 1), along_y(y, x, b_all, -1)
    sibling(("a", 0, 0), y, x, a_all)
    sibling(("b", 0, 0), y, x, b_all)
    xs, ys = {0: x, -1: xm, 1: xp, 2: x2}, {0: y, -1: ym, 1: yp, 2: y2}
    a2, b2 = {}, {}

    def second_a(o):
        a2[o] = (along_y(y, xs[o], a_all, 1), along_y(y, xs[o], a_all, -1))

    def second_b(o):
        b2[o] = (along_x(ys[o], x, b_all, 1), along_x(ys[o], x, b_all, -1))

    second_a(0)
    second_b(0)
    a1p()
    fa_lo = along_x(y, xm, a_lo, 1)
    b1p()
    fb_lo = along_y(ym, x, b_lo, 1)
    a1m()
    fa_hi = along_x(y, xp, a_hi, -1)
    b1m()
    fb_hi = along_y(yp, x, b_hi, -1)
    for o in (-1, 1):
        second_a(o)
        second_b(o)
        sibling(("a", 0, o), y, xs[o], a_all)
        sibling(("b", o, 0), ys[o], x, b_all)

    def done(*chunks):
        for dy, dx in chunks:
            from_sibling[("a", dy, dx)]()
            from_sibling[("b", dy, dx)]()
        return [(ys[dy], xs[dx]) for dy, dx in chunks]

    yield done((0, 0))
    fa_lo()
    fa_hi()
    second_a(2)
    fb_lo()
    fb_hi()
    second_b(2)
    sibling(("a", 0, 2), y, x2, a_all)
    sibling(("b", 2, 0), y2, x, b_all)
    last_a, last_b = {}, {}
    ready = {
        0: [(-1, 0), (1, 0), (0, -1), (0, 1)], -1: [(-1, -1)], 1: [(1, 1), (1, -1), (-1, 1)], 2: [],
    }
    late = []
    for o in (0, -1, 1, 2):
        a2[o][0]()
        lo_a = along_y(ym, xs[o], a_lo, 1)
        b2[o][0]()
        lo_b = along_x(ys[o], xm, b_lo, 1)
        a2[o][1]()
        last_a[o] = (lo_a, along_y(yp, xs[o], a_hi, -1))
        b2[o][1]()
        last_b[o] = (lo_b, along_x(ys[o], xp, b_hi, -1))
        for s in (-1, 1):
            sibling(("a", s, o), ys[s], xs[o], a_all)
            sibling(("b", o, s), ys[o], xs[s], b_all)
        for chunk in late:
            yield done(chunk)
        late = ready[o]
    for chunk in late:
        yield done(chunk)
    late = []
    for o in (0, -1, 1, 2):
        for wait in last_a[o] + last_b[o]:
            wait()
        sibling(("a", 2, o), y2, xs[o], a_all)
        sibling(("b", o, 2), ys[o], x2, b_all)
        for chunk in late:
            yield done(chunk)
        late = [(2, o), (o, 2)] if o != 2 else [(2, 2)]
    for chunk in late:
        yield done(chunk)


GATHER_COPIES = 96


def attend_kernel(q_ref, own_ref, block_ref, bias_ref, out_ref, g, top, total, acc, send, recv, local_sem):
    post = Post(send, recv)
    greet(torus_peers(*here()))

    def merge(keys, bias, first=False):
        q = q_ref[...]
        scores = jnp.concatenate(
            [lax.dot_general(q, k, (((1,), (1,)), ((), ())), preferred_element_type=F32) for k in keys], axis=1
        )
        rows, width = scores.shape
        scores = (scores.reshape(rows // 8, 8, width) * SCORE_SCALE + bias[None]).reshape(rows, width)
        best = jnp.max(scores, axis=1, keepdims=True)
        if not first:
            best = jnp.maximum(best, top[...])
        weights = jnp.exp(scores - best)
        summed = jnp.sum(weights, axis=1, keepdims=True)
        weights = weights.astype(BF16)
        each = width // len(keys)
        mixed = sum(
            jnp.dot(weights[:, i * each : (i + 1) * each], k[:, :LAT], preferred_element_type=F32)
            for i, k in enumerate(keys)
        )
        if first:
            total[...] = summed
            acc[...] = mixed
        else:
            scale = jnp.exp(top[...] - best)
            total[...] = total[...] * scale + summed
            acc[...] = acc[...] * scale + mixed
        top[...] = best

    started = False
    for chunks in gather(post, block_ref, g, 32, local_sem):
        if not started:
            merge([own_ref[...]], bias_ref[16], first=True)
            started = True
        for yy, xx in chunks:
            merge([g[0, yy, xx], g[1, yy, xx]], bias_ref[yy * NX + xx])
    out_ref[...] = (acc[...] / total[...]).astype(BF16)
    post.drain()


def attend(q, own, block, bias):
    rows = q.shape[0]
    return pl.pallas_call(
        attend_kernel,
        out_shape=jax.ShapeDtypeStruct((rows, LAT), BF16),
        in_specs=[pl.BlockSpec(memory_space=pltpu.VMEM)] * 4,
        out_specs=pl.BlockSpec(memory_space=pltpu.VMEM),
        scratch_shapes=[
            pltpu.VMEM((2, NY, NX, NZ * 32, KPAD), BF16),
            pltpu.VMEM((rows, 1), F32),
            pltpu.VMEM((rows, 1), F32),
            pltpu.VMEM((rows, LAT), F32),
            pltpu.SemaphoreType.DMA((GATHER_COPIES,)),
            pltpu.SemaphoreType.DMA((GATHER_COPIES,)),
            pltpu.SemaphoreType.DMA,
        ],
        compiler_params=pltpu.CompilerParams(
            collective_id=0, has_side_effects=True, vmem_limit_bytes=56 * 2**20
        ),
        name="attend",
    )(q, own, block, bias)


def project_kernel(
    ctx_ref, up_ref, proj_hbm, hidden_ref, gain_ref, res_ref, norm_ref,
    ctx_in, proj, other, from_other, parts, parts_in, full,
    local_sem, ctx_send, ctx_recv, send, recv, sib_send, sib_recv,
):
    z, y, x, c = here()
    e = (y * NX + x) * 2 + c
    chip = y * NX + x
    devices = 2 * NX * NY
    chips = NX * NY

    loads = [
        pltpu.make_async_copy(
            proj_hbm.at[:, pl.ds(pl.multiple_of(half * HALF, 128), HALF)], proj.at[i], local_sem.at[i]
        )
        for i, half in enumerate((c, 1 - c))
    ]
    for load in loads:
        load.start()
    barrier = pltpu.get_barrier_semaphore()

    def hello(j, carry):
        pl.semaphore_signal(
            barrier, inc=1, device_id=(z, lax.rem(e + j, devices)), device_id_type=MESH
        )
        return carry

    lax.fori_loop(1, devices, hello, 0)
    pl.semaphore_wait(barrier, devices - 1)

    def ctx_copy(j):
        to = lax.rem(e + j, devices)
        return pltpu.make_async_remote_copy(
            src_ref=ctx_ref.at[to], dst_ref=ctx_in.at[e], send_sem=ctx_send.at[j], recv_sem=ctx_recv.at[j],
            device_id=(z, to), device_id_type=MESH,
        )

    def ctx_arrival(j):
        source = lax.rem(e - j + devices, devices)
        return pltpu.make_async_remote_copy(
            src_ref=ctx_in.at[source], dst_ref=ctx_in.at[source], send_sem=ctx_send.at[j],
            recv_sem=ctx_recv.at[j], device_id=(z, source), device_id_type=MESH,
        )

    def each(low, high, act):
        def body(j, carry):
            act(j)
            return carry

        lax.fori_loop(low, high, body, 0)

    each(1, devices, lambda j: ctx_copy(j).start())
    mine = pltpu.make_async_copy(ctx_ref.at[e], ctx_in.at[e], local_sem.at[2])
    mine.start()
    mine.wait()
    for load in loads:
        load.wait()
    each(1, devices, lambda j: ctx_arrival(j).wait_recv())

    context = ctx_in[...].reshape(devices * 8, LAT)
    first = jnp.dot(context, up_ref[0], preferred_element_type=F32).reshape(chips, 16, 128)
    second = jnp.dot(context, up_ref[1], preferred_element_type=F32).reshape(chips, 16, 128)
    upper = lax.broadcasted_iota(jnp.int32, (chips, 8, 128), 1) < 4

    def swap(v):
        return jnp.concatenate([v[:, 4:], v[:, :4]], axis=1)

    left = jnp.where(upper, first[:, :8], swap(first[:, 8:]))
    right = jnp.where(upper, swap(second[:, :8]), second[:, 8:])
    values = jnp.concatenate([left, right], axis=2).reshape(chips * 8, 256).astype(BF16)

    tile = 640
    for i in range(HALF // tile):
        columns = pl.ds(i * tile, tile)
        part = jnp.dot(values, proj[1, :, columns], preferred_element_type=F32)
        other[:, :, columns] = part.reshape(chips, 8, tile).astype(BF16)
    other[chip] = (other[chip].astype(F32) + hidden_ref[1]).astype(BF16)
    sib = pltpu.make_async_remote_copy(
        src_ref=other, dst_ref=from_other, send_sem=sib_send.at[0], recv_sem=sib_recv.at[0],
        device_id=dev(z, y, x, 1 - c), device_id_type=MESH,
    )
    sib.start()
    for i in range(HALF // tile):
        columns = pl.ds(i * tile, tile)
        part = jnp.dot(values, proj[0, :, columns], preferred_element_type=F32)
        full[:, :, columns] = part.reshape(chips, 8, tile)
    sib.wait()

    def total(j, carry):
        full[j] = full[j] + from_other[j].astype(F32)
        parts[j] = full[j].astype(BF16)
        return carry

    lax.fori_loop(0, chips, total, 0)

    def part_copy(j):
        to = lax.rem(chip + j, chips)
        return pltpu.make_async_remote_copy(
            src_ref=parts.at[to], dst_ref=parts_in.at[j], send_sem=send.at[j], recv_sem=recv.at[j],
            device_id=(z, to * 2 + c), device_id_type=MESH,
        )

    each(1, chips, lambda j: part_copy(j).start())
    res_ref[c] = full[chip] + hidden_ref[0]
    each(1, chips, lambda j: part_copy(j).wait_recv())

    def gathered(j, carry):
        return carry + parts_in[j].astype(F32)

    res_ref[c] = lax.fori_loop(1, chips, gathered, res_ref[c])
    swap_copy = pltpu.make_async_remote_copy(
        src_ref=res_ref.at[c], dst_ref=res_ref.at[c], send_sem=sib_send.at[1], recv_sem=sib_recv.at[1],
        device_id=dev(z, y, x, 1 - c), device_id_type=MESH,
    )
    swap_copy.start()
    swap_in = pltpu.make_async_remote_copy(
        src_ref=res_ref.at[1 - c], dst_ref=res_ref.at[1 - c], send_sem=sib_send.at[1],
        recv_sem=sib_recv.at[1], device_id=dev(z, y, x, 1 - c), device_id_type=MESH,
    )
    swap_in.wait_recv()
    squares = sum(jnp.sum(res_ref[h] * res_ref[h], axis=1, keepdims=True) for h in range(2))
    scale = lax.rsqrt(squares * (1.0 / D) + NORM_EPS)
    norm_ref[...] = (res_ref[c] * scale * gain_ref[c]).astype(BF16)
    swap_copy.wait_send()
    each(1, devices, lambda j: ctx_copy(j).wait_send())
    each(1, chips, lambda j: part_copy(j).wait_send())


def project(ctx, value_up, out_proj, hidden, gain):
    chips = NX * NY
    vmem = pl.BlockSpec(memory_space=pltpu.VMEM)
    return pl.pallas_call(
        project_kernel,
        out_shape=(
            jax.ShapeDtypeStruct((2, 8, HALF), F32),
            jax.ShapeDtypeStruct((8, HALF), BF16),
        ),
        in_specs=[vmem, vmem, pl.BlockSpec(memory_space=pl.ANY), vmem, vmem],
        out_specs=(vmem, vmem),
        scratch_shapes=[
            pltpu.VMEM((2 * chips, 8, LAT), BF16),
            pltpu.VMEM((2, 256, HALF), BF16),
            pltpu.VMEM((chips, 8, HALF), BF16),
            pltpu.VMEM((chips, 8, HALF), BF16),
            pltpu.VMEM((chips, 8, HALF), BF16),
            pltpu.VMEM((chips, 8, HALF), BF16),
            pltpu.VMEM((chips, 8, HALF), F32),
            pltpu.SemaphoreType.DMA((3,)),
            pltpu.SemaphoreType.DMA((2 * chips,)),
            pltpu.SemaphoreType.DMA((2 * chips,)),
            pltpu.SemaphoreType.DMA((chips,)),
            pltpu.SemaphoreType.DMA((chips,)),
            pltpu.SemaphoreType.DMA((2,)),
            pltpu.SemaphoreType.DMA((2,)),
        ],
        compiler_params=pltpu.CompilerParams(
            collective_id=1, has_side_effects=True, vmem_limit_bytes=56 * 2**20
        ),
        name="project",
    )(ctx, value_up, out_proj, hidden, gain)


def ring_sum(post, block, into, pos, n, lo, hi, to):
    plus, minus, far = step(pos, 1, n), step(pos, -1, n), step(pos, 2, n)
    up, down = to(1), to(-1)

    def put(src, i, device):
        return post.put(src, into.at[i], device, into.at[i])

    far_up = put(block(far, lo), 0, up)
    far_down = put(block(far, hi), 1, down)
    free_up = put(block(plus, hi), 2, up)
    free_down = put(block(minus, lo), 3, down)
    yield
    far_up()
    add(block(plus, lo), into.at[0])
    last_up = put(block(plus, lo), 4, up)
    far_down()
    add(block(minus, hi), into.at[1])
    last_down = put(block(minus, hi), 5, down)
    yield
    free_up()
    last_down()
    add(block(pos, hi), into.at[2], into.at[5])
    free_down()
    last_up()
    add(block(pos, lo), into.at[3], into.at[4])


def add(ref, *others):
    if len(ref.shape) == 3:
        for i in range(ref.shape[0]):
            add(ref.at[i], *[o.at[i] for o in others])
        return
    value = ref[...].astype(F32)
    for o in others:
        value = value + o[...].astype(F32)
    ref[...] = value.astype(BF16)


MOE_COPIES = 144


def moe_kernel(
    norm_ref, table_ref, gate_hbm, up_hbm, down_hbm, out_ref,
    block, g, gate, up, down, hidden, other, from_other, sums, ring_a, ring_b, ring_c, ring_d, z_in, final,
    send, recv, local_sem,
):
    z, y, x, c = here()
    loads = [
        pltpu.make_async_copy(gate_hbm.at[0], gate, local_sem.at[1]),
        pltpu.make_async_copy(up_hbm.at[0], up, local_sem.at[2]),
    ] + [
        pltpu.make_async_copy(
            down_hbm.at[0, :, pl.ds(pl.multiple_of(half * HALF, 128), HALF)], down.at[i], local_sem.at[3 + i]
        )
        for i, half in enumerate((c, 1 - c))
    ]
    for load in loads:
        load.start()
    post = Post(send, recv)
    greet(torus_peers(z, y, x, c))
    block[:, :HALF] = norm_ref[...]
    block[:, HALF:] = table_ref[...]
    for _ in gather(post, block, g, 8, local_sem.at[0]):
        pass
    for load in loads:
        load.wait()

    e = (y * NX + x) * 2 + c
    ours = (lax.broadcasted_iota(jnp.int32, (256, TABLE), 1) == e).astype(F32)

    def hidden_rows(i, carry):
        rows = [g[h, i].reshape(256, HALF + TABLE) for h in range(2)]
        weight = jnp.sum(
            (rows[0][:, HALF:].astype(F32) + rows[1][:, HALF:].astype(F32)) * ours, axis=1, keepdims=True
        )

        def product(w):
            return jnp.dot(rows[0][:, :HALF], w[:HALF], preferred_element_type=F32) + jnp.dot(
                rows[1][:, :HALF], w[HALF:], preferred_element_type=F32
            )

        gated = product(gate)
        raised = product(up)
        hidden[i] = (gated / (1.0 + jnp.exp(-gated)) * raised * weight).astype(BF16)
        return carry

    lax.fori_loop(0, NY, hidden_rows, 0)

    xs = [step(x, o, NX) for o in range(NX)]
    ys = [step(y, o, NY) for o in range(NY)]
    tile = 640
    order = (ys[2], ys[1], ys[3], ys[0])
    waits = []
    for yy in order:
        rows = hidden[yy]
        for i in range(HALF // tile):
            columns = pl.ds(i * tile, tile)
            part = jnp.dot(rows, down[1, :, columns], preferred_element_type=F32)
            other[yy, :, :, columns] = part.reshape(NX, 64, tile).astype(BF16)
        waits.append(post.put(other.at[yy], from_other.at[yy], dev(z, y, x, 1 - c), from_other.at[yy]))
    for yy, wait in zip(order, waits):
        wait()
        rows = hidden[yy]
        for i in range(HALF // tile):
            columns = pl.ds(i * tile, tile)
            part = jnp.dot(rows, down[0, :, columns], preferred_element_type=F32).reshape(NX, 64, tile)
            sums[yy, :, :, columns] = (part + from_other[yy, :, :, columns].astype(F32)).astype(BF16)

    a_lo, a_hi, b_lo, b_hi = [pl.ds(16 * i, 16) for i in range(4)]

    def to_x(s):
        return dev(z, y, step(x, s, NX), c)

    def to_y(s):
        return dev(z, step(y, s, NY), x, c)

    def together(*rings):
        for _ in zip(*rings):
            pass
        for ring in rings:
            for _ in ring:
                pass

    together(
        ring_sum(post, lambda p, r: sums.at[p, :, r], ring_a, y, NY, a_lo, a_hi, to_y),
        ring_sum(post, lambda p, r: sums.at[:, p, r], ring_b, x, NX, b_lo, b_hi, to_x),
    )
    together(
        ring_sum(post, lambda p, r: sums.at[y, p, r], ring_c, x, NX, a_lo, a_hi, to_x),
        ring_sum(post, lambda p, r: sums.at[p, x, r], ring_d, y, NY, b_lo, b_hi, to_y),
    )

    def zrows(at):
        return pl.ds(pl.multiple_of(at * 8, 8), 8)

    waits = [
        post.put(sums.at[y, x, zrows(step(z, j, NZ))], z_in.at[j], dev(step(z, j, NZ), y, x, c), z_in.at[j])
        for j in range(1, NZ)
    ]
    keep = pltpu.make_async_copy(sums.at[y, x, zrows(z)], z_in.at[0], local_sem.at[0])
    keep.start()
    keep.wait()
    for wait in waits:
        wait()
    value = z_in[0].astype(F32)
    for j in range(1, NZ):
        value = value + z_in[j].astype(F32)
    final[c] = value
    post.put(final.at[c], final.at[c], dev(z, y, x, 1 - c), final.at[1 - c])()
    upper = lax.broadcasted_iota(jnp.int32, (4, HALF), 0) * 0 + c == 0
    for h in range(2):
        out_ref[:, h * HALF : (h + 1) * HALF] = jnp.where(upper, final[h, :4], final[h, 4:])
    post.drain()


def moe(normed, table, gate_proj, up_proj, down_proj):
    vmem = pl.BlockSpec(memory_space=pltpu.VMEM)
    hbm = pl.BlockSpec(memory_space=pl.ANY)
    return pl.pallas_call(
        moe_kernel,
        out_shape=jax.ShapeDtypeStruct((4, D), F32),
        in_specs=[vmem, vmem, hbm, hbm, hbm],
        out_specs=vmem,
        scratch_shapes=[
            pltpu.VMEM((8, HALF + TABLE), BF16),
            pltpu.VMEM((2, NY, NX, NZ * 8, HALF + TABLE), BF16),
            pltpu.VMEM((D, FFG), BF16),
            pltpu.VMEM((D, FFG), BF16),
            pltpu.VMEM((2, FFG, HALF), BF16),
            pltpu.VMEM((NY, 256, FFG), BF16),
            pltpu.VMEM((NY, NX, 64, HALF), BF16),
            pltpu.VMEM((NY, NX, 64, HALF), BF16),
            pltpu.VMEM((NY, NX, 64, HALF), BF16),
            pltpu.VMEM((6, NX, 16, HALF), BF16),
            pltpu.VMEM((6, NY, 16, HALF), BF16),
            pltpu.VMEM((6, 16, HALF), BF16),
            pltpu.VMEM((6, 16, HALF), BF16),
            pltpu.VMEM((NZ, 8, HALF), BF16),
            pltpu.VMEM((2, 8, HALF), F32),
            pltpu.SemaphoreType.DMA((MOE_COPIES,)),
            pltpu.SemaphoreType.DMA((MOE_COPIES,)),
            pltpu.SemaphoreType.DMA((5,)),
        ],
        compiler_params=pltpu.CompilerParams(
            collective_id=2, has_side_effects=True, vmem_limit_bytes=56 * 2**20
        ),
        name="moe",
    )(normed, table, gate_proj, up_proj, down_proj)


def per_device(
    hidden_in, query, prefix_pool, suffix_cache, block_list, prefix_count, suffix_count, value_up,
    out_proj, norm_gain, expert_ids, gate_weights, gate_proj, up_proj, down_proj,
):
    e = lax.axis_index("expert")
    core, chip = lax.rem(e, 2), lax.div(e, 2)

    half = BLOCK // 2 * KDIM
    block = lax.dynamic_slice(prefix_pool, (chip, core * half), (1, half)).reshape(BLOCK // 2, KDIM)
    block = jnp.pad(block, ((0, 0), (0, KPAD - KDIM)))
    q = query.reshape(4, 32, 2, KDIM).transpose(1, 2, 0, 3).reshape(256, KDIM)
    q = jnp.pad(q, ((0, 0), (0, KPAD - KDIM)))
    own = jnp.pad(suffix_cache.reshape(4 * SUFFIX, KDIM), ((0, 0), (0, KPAD - KDIM)))
    in_prefix = jnp.arange(32, dtype=jnp.int32)[None, :] < prefix_count[:, None]
    listed = jnp.where(in_prefix, block_list, -1)
    member = jnp.any(listed[:, :, None] == jnp.arange(128, dtype=jnp.int32), axis=1)
    member = member.reshape(4, NZ, 16).transpose(2, 0, 1)
    pool_live = jnp.broadcast_to(member[:, None, :, None, :, None], (16, 2, 4, 2, NZ, 32)).reshape(16, 8, 512)
    row = jnp.arange(4 * SUFFIX, dtype=jnp.int32)
    own_live = (row // SUFFIX == jnp.arange(4, dtype=jnp.int32)[:, None]) & (
        row % SUFFIX < suffix_count[:, None]
    )
    own_live = jnp.concatenate([own_live, own_live], axis=0)
    bias = jnp.where(jnp.concatenate([pool_live, own_live[None]], axis=0), 0.0, NEG_FILL).astype(F32)
    context = attend(q, own, block, bias)

    mine = (jnp.arange(8, dtype=jnp.int32) // 4 == core)[:, None]
    hidden = jnp.where(mine, jnp.concatenate([hidden_in, hidden_in], axis=0).astype(F32), 0.0)
    hidden = hidden.reshape(8, 2, HALF).transpose(1, 0, 2)
    hidden = jnp.where(core == 0, hidden, hidden[::-1])
    gain = norm_gain.astype(F32).reshape(2, 1, HALF)
    residual, normed = project(context.reshape(32, 8, LAT), value_up, out_proj, hidden, gain)
    residual_out = lax.dynamic_slice(residual, (0, core * 4, 0), (2, 4, HALF)).transpose(1, 0, 2).reshape(4, D)

    named = expert_ids[:, :, None] == jnp.arange(TABLE, dtype=jnp.int32)
    table = jnp.sum(jnp.where(named, gate_weights.astype(F32)[:, :, None], 0.0), axis=1)
    table = jnp.where(mine, jnp.concatenate([table, table], axis=0), 0.0).astype(BF16)
    return residual_out, moe(normed, table, gate_proj, up_proj, down_proj)


def solution(mesh):
    rows = P(("dp", "expert"), None)
    in_specs = (
        rows, rows, P("dp", None), rows, rows, P(("dp", "expert")), P(("dp", "expert")),
        P("expert", None, None), P("expert", None), P(), rows, rows,
        P("expert", None, "dp"), P("expert", None, "dp"), P("expert", "dp", None),
    )
    return jax.shard_map(
        per_device, mesh=mesh, in_specs=in_specs, out_specs=(rows, rows), check_vma=False
    )
```

time: 614 us -> 214 us (0.35)
  the two profiles are of different devices: /device:TPU:2 before, /device:TPU:1 now
where the time goes in v1:
time: 214 us; the launch traced here: 213 us
  Pallas kernels  190 us (89%)
  local copies, waits for them, and re-layouts  16.5 us (8%)
  other arithmetic  6.14 us (3%)
    pallas_call x1, Pallas kernels, moe(): pl.pallas_call(moe_kernel, out_shape=jax.ShapeDtypeStruct((4, D), F32), i...  108 us
    pallas_call x1, Pallas kernels, attend(): pl.pallas_call(attend_kernel, out_shape=jax.ShapeDtypeStruct((rows, LAT),...  55.3 us
    pallas_call x1, Pallas kernels, project(): pl.pallas_call(project_kernel, out_shape=(jax.ShapeDtypeStruct((2, 8, HAL...  26.6 us
    unnamed x12, local copies, waits for them, and re-layouts  9.14 us

profile of v1, /device:TPU:1, one launch (start us, length us, event | category | flops | bytes accessed | tf_op | source)
XLA Modules:
  0.0 213.2 jit_solution(17592215906466817488)
XLA Ops:
  0.7 0.9 fusion.10
  1.8 0.8 copy.26
  2.6 0.8 copy.27
  3.5 0.7 fusion.2.table_ref
  4.1 0.7 fusion.1
  4.9 1.3 reshape.93
  6.2 0.3 dynamic-slice_reduce_fusion
  6.6 0.6 pad.14.block_ref
  7.2 0.9 select_bitcast_fusion
  8.2 0.7 reverse_select_fusion.hidden_ref
  9.0 0.5 reshape.88
  9.5 0.8 add_select_fusion.bias_ref
  10.3 0.4 reshape.83
  10.7 0.3 copy.31
  11.1 0.8 pad.12.q_ref
  11.9 0.7 reshape.85
  12.5 0.9 pad.13.own_ref
  13.4 55.3 %attend.1 = bf16[256,512]{1,0:T(8,128)(2,1)} custom-call(bf16[256,640]{1,0:T(8,128)(2,1)} %pad.12.q_ref, bf16[512,640]{1,0:T(8,128)(2,1)} %pad.13.own_ref, bf16[32,640]{1,0:T(8,128)(2,1)} %pad.14.block_ref, f32[17,8,512]{2,1,0:T(8,128)} %add_select_fusion.bias_ref), custom_call_target="tpu_custom_call" | custom-call | tf_op jit(solution)/shard_map/attend/pallas_call | solution.py:255
  68.7 26.6 %project.1 = (f32[2,8,2560]{2,1,0:T(8,128)}, bf16[8,2560]{1,0:T(8,128)(2,1)}) custom-call(bf16[32,8,512]{2,1,0:T(8,128)(2,1)} %bitcast.17, bf16[2,512,128]{2,1,0:T(8,128)(2,1)} %up_ref.1, bf16[256,5120]{1,0:T(8,128)(2,1)} %proj_hbm.1, f32[2,8,2560]{2,1,0:T(8,128)} %reverse_select_fusion.hidden_ref, f32[2,1,2560]{2,1,0:T(1,128)} %bitcast.18), custom_call_target="tpu_custom_call" | custom-call | tf_op jit(solution)/shard_map/project/pallas_call | solution.py:407
  95.3 1.6 constant_dynamic-slice_fusion
  96.9 2.5 %copy.28.gate_hbm = bf16[1,5120,192]{2,1,0:T(8,128)(2,1)} copy(bf16[1,5120,192]{1,2,0:T(8,128)(2,1)S(1)} %copy-done.1) | data formatting | bytes 3932160 | tf_op args[12]
  99.4 4.3 %copy.29.up_hbm = bf16[1,5120,192]{2,1,0:T(8,128)(2,1)} copy(bf16[1,5120,192]{1,2,0:T(8,128)(2,1)} %param.28) | data formatting | bytes 3932160 | tf_op args[13]
  103.7 107.9 %moe.1 = f32[4,5120]{1,0:T(4,128)} custom-call(bf16[8,2560]{1,0:T(8,128)(2,1)} %get-tuple-element.5.norm_ref, bf16[8,128]{1,0:T(8,128)(2,1)} %fusion.2.table_ref, bf16[1,5120,192]{2,1,0:T(8,128)(2,1)} %copy.28.gate_hbm, bf16[1,5120,192]{2,1,0:T(8,128)(2,1)} %copy.29.up_hbm, bf16[1,192,5120]{2,1,0:T(8,128)(2,1)} %down_hbm.1), custom_call_target="tpu_custom_call" | custom-call | tf_op jit(solution)/shard_map/moe/pallas_call | solution.py:596
  211.6 1.5 copy.33
  (18 shorter events, 0.8 us)
Async XLA Ops:
  0.6 5.6 %copy-start = (bf16[16,36864]{1,0:T(8,128)(2,1)S(1)}, bf16[16,36864]{1,0:T(8,128)(2,1)}, u32[]{:S(2)}) copy-start(bf16[16,36864]{1,0:T(8,128)(2,1)} %param.17) | copy-start | bytes 3538948
  0.6 9.6 %copy-start.3 = (bf16[4,36864]{1,0:T(4,128)(2,1)S(1)}, bf16[4,36864]{1,0:T(4,128)(2,1)}, u32[]{:S(2)}) copy-start(bf16[4,36864]{1,0:T(4,128)(2,1)} %param.16) | copy-start | bytes 884740
  8.2 3.7 %copy-start.2 = (bf16[4,73728]{1,0:T(4,128)(2,1)S(1)}, bf16[4,73728]{1,0:T(4,128)(2,1)}, u32[]{:S(2)}) copy-start(bf16[4,73728]{1,0:T(4,128)(2,1)} %param.18) | copy-start | bytes 1769476
  68.7 28.2 %copy-start.1 = (bf16[1,5120,192]{1,2,0:T(8,128)(2,1)S(1)}, bf16[1,5120,192]{1,2,0:T(8,128)(2,1)}, u32[]{:S(2)}) copy-start(bf16[1,5120,192]{1,2,0:T(8,128)(2,1)} %param.27) | copy-start | bytes 5898244

commit v2 on v1

v2 whole, which is shorter than its diff:
```python
import functools
import jax
import jax.numpy as jnp
from jax import lax
from jax.experimental import pallas as pl
from jax.experimental.pallas import tpu as pltpu
from jax.sharding import PartitionSpec as P

HEADS = 64
LAT = 512
BLOCK = 64
SUFFIX = 128
KDIM = 576
KPAD = 640
D = 5120
HALF = 2560
FFG = 192
TABLE = 128

NEG_FILL = -1e30
SCORE_SCALE = 192.0 ** (-0.5)
NORM_EPS = 1e-06

NX, NY, NZ = 4, 4, 8
MESH = pl.DeviceIdType.MESH
F32 = jnp.float32
BF16 = jnp.bfloat16


def here():
    z = lax.axis_index("dp")
    e = lax.axis_index("expert")
    core = lax.rem(e, 2)
    chip = lax.div(e, 2)
    return z, lax.div(chip, NX), lax.rem(chip, NX), core


def dev(z, y, x, core):
    return (z, (y * NX + x) * 2 + core)


def step(v, by, n):
    return lax.rem(v + by + n, n)


class Post:
    def __init__(self, send, recv):
        self.send, self.recv, self.count, self.sent = send, recv, 0, []

    def put(self, src, dst, to, lands):
        i = self.count
        self.count += 1
        copy = pltpu.make_async_remote_copy(
            src_ref=src, dst_ref=dst, send_sem=self.send.at[i], recv_sem=self.recv.at[i],
            device_id=to, device_id_type=MESH,
        )
        copy.start()
        self.sent.append(copy)
        return pltpu.make_async_remote_copy(
            src_ref=lands, dst_ref=lands, send_sem=self.send.at[i], recv_sem=self.recv.at[i],
            device_id=to, device_id_type=MESH,
        ).wait_recv

    def drain(self):
        for copy in self.sent:
            copy.wait_send()


def gather(post, block, g, local_sem):
    z, y, x, c = here()
    xs = {o: step(x, o, NX) for o in (0, -1, 1, 2)}
    ys = {o: step(y, o, NY) for o in (0, -1, 1, 2)}
    zs = {o: step(z, o, NZ) for o in range(-4, 5)}
    other = dev(z, y, x, 1 - c)

    def move(view, arriving, to):
        return post.put(view, view, to, arriving)

    block_ab, block_c = block
    whole = g.c_block is None
    keeps = [
        pltpu.make_async_copy(block_ab, g.ab(c, y, x, z, 1), local_sem.at[0]),
        pltpu.make_async_copy(block_c, g.c_slab(c, z) if whole else g.c_block(c, y, x, z), local_sem.at[1]),
    ]
    for keep in keeps:
        keep.start()
    c_x = [] if whole else [
        post.put(block_c, g.c_block(c, y, x, z), dev(z, y, step(x, o, NX), c), g.c_block(c, y, step(x, -o, NX), z))
        for o in (1, 3, 2)
    ]
    ab_z = [
        post.put(block_ab, g.ab(c, y, x, z, 1), dev(step(z, j, NZ), y, x, c), g.ab(c, y, x, step(z, -j, NZ), 1))
        for j in (1, 7, 2, 6, 3, 5, 4)
    ]
    for keep in keeps:
        keep.wait()
    from_sibling = {}

    def sibling_c(dz):
        from_sibling[dz] = move(g.c_slab(c, zs[dz]), g.c_slab(1 - c, zs[dz]), other)

    def along_z(dz, by, part):
        return move(g.c_slab(c, zs[dz], part), g.c_slab(c, zs[dz - by], part), dev(zs[by], y, x, c))

    up, down = {}, {}

    def begin_z():
        for part in range(PARTS):
            up[part], down[PARTS - 1 - part] = along_z(0, 1, part), along_z(0, -1, PARTS - 1 - part)
        sibling_c(0)

    ring_events = [(s, part) for s in (1, 2, 3) for part in range(PARTS)]

    def ring_z(events):
        for _ in range(events):
            s, part = ring_events.pop(0)
            up[part]()
            if s < 3 or part < PARTS // 2:
                up[part] = along_z(-s, 1, part)
            back = PARTS - 1 - part
            down[back]()
            if s < 3 or back >= PARTS // 2:
                down[back] = along_z(s, -1, back)
            if part == PARTS - 1:
                sibling_c(-s)
                sibling_c(s)

    for wait in c_x:
        wait()
    c_y = [] if whole else [
        move(g.c_row(c, y, z), g.c_row(c, step(y, -o, NY), z), dev(z, step(y, o, NY), x, c)) for o in (1, 3, 2)
    ]
    if whole:
        begin_z()
    yield []
    for wait in ab_z:
        wait()

    halves = {"a": (0, 4), "b": (4, 4), "a_lo": (0, 2), "a_hi": (2, 2), "b_lo": (4, 2), "b_hi": (6, 2)}
    def sibling(name, dy, dx):
        yy, xx = ys[dy], xs[dx]
        from_sibling[(name, dy, dx)] = move(g.ab(c, yy, xx, *halves[name]), g.ab(1 - c, yy, xx, *halves[name]), other)

    def along_x(dy, dx, name, by):
        yy, xx = ys[dy], xs[dx]
        return move(
            g.ab(c, yy, xx, *halves[name]), g.ab(c, yy, step(xx, -by, NX), *halves[name]), dev(z, y, xs[by], c)
        )

    def along_y(dy, dx, name, by):
        yy, xx = ys[dy], xs[dx]
        return move(
            g.ab(c, yy, xx, *halves[name]), g.ab(c, step(yy, -by, NY), xx, *halves[name]), dev(z, ys[by], x, c)
        )

    a1p, b1p = along_x(0, 0, "a", 1), along_y(0, 0, "b", 1)
    a1m, b1m = along_x(0, 0, "a", -1), along_y(0, 0, "b", -1)
    sibling("a", 0, 0)
    sibling("b", 0, 0)
    a2, b2 = {}, {}

    def second(o):
        a2[o] = (along_y(0, o, "a", 1), along_y(0, o, "a", -1))
        b2[o] = (along_x(o, 0, "b", 1), along_x(o, 0, "b", -1))

    second(0)
    if not whole:
        for wait in c_y:
            wait()
        begin_z()
    else:
        ring_z(PARTS)
    a1p()
    fa_lo = along_x(0, -1, "a_lo", 1)
    b1p()
    fb_lo = along_y(-1, 0, "b_lo", 1)
    a1m()
    fa_hi = along_x(0, 1, "a_hi", -1)
    b1m()
    fb_hi = along_y(1, 0, "b_hi", -1)
    for o in (-1, 1):
        second(o)
        sibling("a", 0, o)
        sibling("b", o, 0)

    def done(*parts):
        ready = []
        for part in parts:
            if isinstance(part, int):
                from_sibling[part]()
                ready.append((zs[part],))
            else:
                from_sibling[("a",) + part]()
                from_sibling[("b",) + part]()
                ready.append((ys[part[0]], xs[part[1]]))
        return ready

    queue = [(0, 0), 0]

    def some():
        return done(queue.pop(0)) if queue else []

    yield some()
    ring_z(PARTS)
    yield some()
    fa_lo()
    fa_hi()
    fb_lo()
    fb_hi()
    second(2)
    sibling("a", 0, 2)
    sibling("b", 2, 0)

    last_a, last_b = {}, {}
    ready = {
        0: [(-1, 0), (1, 0), (0, -1), (0, 1)], -1: [(-1, -1)], 1: [(1, 1), (1, -1), (-1, 1)], 2: [],
    }
    seen = 0
    for o in (0, -1, 1, 2):
        ring_z(min(PARTS // 2, len(ring_events)))
        yield some()
        a2[o][0]()
        lo_a = along_y(-1, o, "a_lo", 1)
        b2[o][0]()
        lo_b = along_x(o, -1, "b_lo", 1)
        yield some()
        a2[o][1]()
        last_a[o] = (lo_a, along_y(1, o, "a_hi", -1))
        b2[o][1]()
        last_b[o] = (lo_b, along_x(o, 1, "b_hi", -1))
        for side in (-1, 1):
            sibling("a", side, o)
            sibling("b", o, side)
        yield some()
        now = 3 - -(-len(ring_events) // PARTS)
        queue += ready[o] + [d for n in range(seen + 1, now + 1) for d in (-n, n)]
        seen = now
    for o in (0, -1, 1, 2):
        for wait in last_a[o]:
            wait()
        sibling("a", 2, o)
        yield some()
        for wait in last_b[o]:
            wait()
        sibling("b", o, 2)
        yield some()
        queue += [(2, o), (o, 2)] if o != 2 else [(2, 2)]
    for part in range(PARTS // 2):
        up[part]()
        down[PARTS - 1 - part]()
    sibling_c(4)
    queue += [4]
    while queue:
        yield some()


COPIES = 400
PARTS = 4


class Pool:
    AB, C = 24, 128
    c_block = None

    def __init__(self, ab, c):
        self.g_ab, self.g_c = ab, c

    def ab(self, core, yy, xx, z0, nz):
        return self.g_ab.at[core, yy, xx, pl.ds(z0, nz)]

    def c_slab(self, core, zz, part=None):
        if part is None:
            return self.g_c.at[core, zz]
        return self.g_c.at[core, zz, pl.ds(part * (self.C // PARTS), self.C // PARTS)]


class Tokens:
    AB, C = 1664, 1024

    def __init__(self, g):
        self.g = g

    def rows(self, z0, nz):
        return pl.ds(pl.multiple_of(z0 * 8, 8), nz * 8)

    def ab(self, core, yy, xx, z0, nz):
        return self.g.at[core, yy, xx, self.rows(z0, nz), pl.ds(0, self.AB)]

    def c_block(self, core, yy, xx, zz):
        return self.g.at[core, yy, xx, self.rows(zz, 1), pl.ds(self.AB, self.C)]

    def c_row(self, core, yy, zz):
        return self.g.at[core, yy, :, self.rows(zz, 1), pl.ds(self.AB, self.C)]

    def c_slab(self, core, zz, part=None):
        ys = pl.ds(0, NY) if part is None else pl.ds(part * (NY // PARTS), NY // PARTS)
        return self.g.at[core, ys, :, self.rows(zz, 1), pl.ds(self.AB, self.C)]


def attend_part(
    post, q_ref, own_ref, block_ab_ref, block_c_ref, own_bias_ref, ab_bias_ref, c_bias_ref, out_ref,
    g_ab, g_c, top, total, acc, local_sem,
):
    def merge(keys, bias, first=False):
        q = q_ref[...]
        scores = lax.dot_general(q, keys, (((1,), (1,)), ((), ())), preferred_element_type=F32)
        rows, width = scores.shape
        scores = (scores.reshape(rows // 8, 8, width) * SCORE_SCALE + bias[None]).reshape(rows, width)
        best = jnp.max(scores, axis=1, keepdims=True)
        if not first:
            best = jnp.maximum(best, top[...])
        weights = jnp.exp(scores - best)
        summed = jnp.sum(weights, axis=1, keepdims=True)
        mixed = jnp.dot(weights.astype(BF16), keys[:, :LAT], preferred_element_type=F32)
        if first:
            total[...] = summed
            acc[...] = mixed
        else:
            scale = jnp.exp(top[...] - best)
            total[...] = total[...] * scale + summed
            acc[...] = acc[...] * scale + mixed
        top[...] = best

    pool = Pool(g_ab, g_c)
    block = block_ab_ref, block_c_ref
    started = False
    for parts in gather(post, block, pool, local_sem):
        if not started:
            merge(own_ref[...], own_bias_ref[...], first=True)
            started = True
        for part in parts:
            if len(part) == 2:
                yy, xx = part
                keys = jnp.concatenate([g_ab[h, yy, xx].reshape(NZ * Pool.AB, KPAD) for h in range(2)], axis=0)
                merge(keys, ab_bias_ref[yy * NX + xx])
            else:
                keys = jnp.concatenate([g_c[0, part[0]], g_c[1, part[0]]], axis=0)
                merge(keys, c_bias_ref[part[0]])
    out_ref[...] = (acc[...] / total[...]).reshape(out_ref.shape).astype(BF16)


def both_halves(v, c):
    v = jnp.concatenate([v, v], axis=0)
    return jnp.where(lax.broadcasted_iota(jnp.int32, v.shape, 0) // 4 == c, v, 0.0)


def own_rows(out_ref, halves, c):
    upper = lax.broadcasted_iota(jnp.int32, (4, HALF), 0) * 0 + c == 0
    for h in range(2):
        out_ref[:, h * HALF : (h + 1) * HALF] = jnp.where(upper, halves[h, :4], halves[h, 4:])


def project_part(
    ctx_ref, up_ref, hidden_ref, gain_ref, norm_ref,
    ctx_in, proj, other, from_other, parts, parts_in, full, res_ref, loads,
    local_sem, ctx_send, ctx_recv, send, recv, sib_send, sib_recv,
):
    z, y, x, c = here()
    e = (y * NX + x) * 2 + c
    chip = y * NX + x
    devices = 2 * NX * NY
    chips = NX * NY

    def ctx_copy(j):
        to = lax.rem(e + j, devices)
        return pltpu.make_async_remote_copy(
            src_ref=ctx_ref.at[to], dst_ref=ctx_in.at[e], send_sem=ctx_send.at[j], recv_sem=ctx_recv.at[j],
            device_id=(z, to), device_id_type=MESH,
        )

    def ctx_arrival(j):
        source = lax.rem(e - j + devices, devices)
        return pltpu.make_async_remote_copy(
            src_ref=ctx_in.at[source], dst_ref=ctx_in.at[source], send_sem=ctx_send.at[j],
            recv_sem=ctx_recv.at[j], device_id=(z, source), device_id_type=MESH,
        )

    def each(low, high, act):
        def body(j, carry):
            act(j)
            return carry

        lax.fori_loop(low, high, body, 0)

    each(1, devices, lambda j: ctx_copy(j).start())
    mine = pltpu.make_async_copy(ctx_ref.at[e], ctx_in.at[e], local_sem)
    mine.start()
    mine.wait()
    for load in loads:
        load.wait()
    each(1, devices, lambda j: ctx_arrival(j).wait_recv())

    context = ctx_in[...].reshape(devices * 8, LAT)
    first = jnp.dot(context, up_ref[0], preferred_element_type=F32).reshape(chips, 16, 128)
    second = jnp.dot(context, up_ref[1], preferred_element_type=F32).reshape(chips, 16, 128)
    upper = lax.broadcasted_iota(jnp.int32, (chips, 8, 128), 1) < 4

    def swap(v):
        return jnp.concatenate([v[:, 4:], v[:, :4]], axis=1)

    left = jnp.where(upper, first[:, :8], swap(first[:, 8:]))
    right = jnp.where(upper, swap(second[:, :8]), second[:, 8:])
    values = jnp.concatenate([left, right], axis=2).reshape(chips * 8, 256).astype(BF16)

    tile = 640
    for i in range(HALF // tile):
        columns = pl.ds(i * tile, tile)
        part = jnp.dot(values, proj[1, :, columns], preferred_element_type=F32)
        other[:, :, columns] = part.reshape(chips, 8, tile).astype(BF16)
    hidden = both_halves(hidden_ref[...].astype(F32), c)
    first_half = lax.broadcasted_iota(jnp.int32, (8, HALF), 0) * 0 + c == 0
    hidden_own = jnp.where(first_half, hidden[:, :HALF], hidden[:, HALF:])
    hidden_other = jnp.where(first_half, hidden[:, HALF:], hidden[:, :HALF])
    other[chip] = (other[chip].astype(F32) + hidden_other).astype(BF16)
    sib = pltpu.make_async_remote_copy(
        src_ref=other, dst_ref=from_other, send_sem=sib_send.at[0], recv_sem=sib_recv.at[0],
        device_id=dev(z, y, x, 1 - c), device_id_type=MESH,
    )
    sib.start()
    for i in range(HALF // tile):
        columns = pl.ds(i * tile, tile)
        part = jnp.dot(values, proj[0, :, columns], preferred_element_type=F32)
        full[:, :, columns] = part.reshape(chips, 8, tile)
    sib.wait()

    def total(j, carry):
        full[j] = full[j] + from_other[j].astype(F32)
        parts[j] = full[j].astype(BF16)
        return carry

    lax.fori_loop(0, chips, total, 0)

    def part_copy(j):
        to = lax.rem(chip + j, chips)
        return pltpu.make_async_remote_copy(
            src_ref=parts.at[to], dst_ref=parts_in.at[j], send_sem=send.at[j], recv_sem=recv.at[j],
            device_id=(z, to * 2 + c), device_id_type=MESH,
        )

    each(1, chips, lambda j: part_copy(j).start())
    res_ref[c] = full[chip] + hidden_own
    each(1, chips, lambda j: part_copy(j).wait_recv())

    def gathered(j, carry):
        return carry + parts_in[j].astype(F32)

    res_ref[c] = lax.fori_loop(1, chips, gathered, res_ref[c])
    swap_copy = pltpu.make_async_remote_copy(
        src_ref=res_ref.at[c], dst_ref=res_ref.at[c], send_sem=sib_send.at[1], recv_sem=sib_recv.at[1],
        device_id=dev(z, y, x, 1 - c), device_id_type=MESH,
    )
    swap_copy.start()
    swap_in = pltpu.make_async_remote_copy(
        src_ref=res_ref.at[1 - c], dst_ref=res_ref.at[1 - c], send_sem=sib_send.at[1],
        recv_sem=sib_recv.at[1], device_id=dev(z, y, x, 1 - c), device_id_type=MESH,
    )
    swap_in.wait_recv()
    squares = sum(jnp.sum(res_ref[h] * res_ref[h], axis=1, keepdims=True) for h in range(2))
    scale = lax.rsqrt(squares * (1.0 / D) + NORM_EPS)
    norm_ref[...] = (res_ref[c] * scale * gain_ref[c].astype(F32)).astype(BF16)

    def finish():
        swap_copy.wait_send()
        each(1, devices, lambda j: ctx_copy(j).wait_send())
        each(1, chips, lambda j: part_copy(j).wait_send())

    return finish


def add(ref, *others):
    if len(ref.shape) > 2:
        for i in range(ref.shape[0]):
            add(ref.at[i], *[o.at[i] for o in others])
        return
    value = ref[...].astype(F32)
    for o in others:
        value = value + o[...].astype(F32)
    ref[...] = value.astype(BF16)


class Ring4:
    def __init__(self, post, block, into, pos, lo, hi, to):
        self.post, self.block, self.into, self.lo, self.hi = post, block, into, lo, hi
        self.pos, self.plus, self.minus, self.far_at = pos, step(pos, 1, 4), step(pos, -1, 4), step(pos, 2, 4)
        self.up, self.down = to(1), to(-1)

    def put(self, src, i, device):
        return self.post.put(src, self.into.at[i], device, self.into.at[i])

    def far(self):
        self.far_up = self.put(self.block(self.far_at, self.lo), 0, self.up)
        self.far_down = self.put(self.block(self.far_at, self.hi), 1, self.down)

    def near(self):
        self.free_up = self.put(self.block(self.plus, self.hi), 2, self.up)
        self.free_down = self.put(self.block(self.minus, self.lo), 3, self.down)

    def last(self):
        self.far_up()
        add(self.block(self.plus, self.lo), self.into.at[0])
        self.last_up = self.put(self.block(self.plus, self.lo), 4, self.up)
        self.far_down()
        add(self.block(self.minus, self.hi), self.into.at[1])
        self.last_down = self.put(self.block(self.minus, self.hi), 5, self.down)

    def finish(self):
        self.free_up()
        self.last_down()
        add(self.block(self.pos, self.hi), self.into.at[2], self.into.at[5])
        self.free_down()
        self.last_up()
        add(self.block(self.pos, self.lo), self.into.at[3], self.into.at[4])


def ring8(post, sums, into, z, y, x, c):
    up_to, down_to = dev(step(z, 1, NZ), y, x, c), dev(step(z, -1, NZ), y, x, c)
    count = 0

    def half(dz, h):
        return sums.at[step(z, dz, NZ), pl.ds(2 * h, 2)]

    def put(dz, h):
        nonlocal count
        i = count
        count += 1
        return post.put(half(dz, h), into.at[i], up_to if dz > 0 else down_to, into.at[i]), into.at[i]

    up, down = [None, None], [None, None]
    up[0] = put(4, 0)
    down[1] = post.put(half(4, 1), into.at[count], down_to, into.at[count]), into.at[count]
    count += 1
    up[1], down[0] = put(3, 1), put(-3, 0)
    yield
    for dz in (3, 2, 1):
        for h_up in (0, 1):
            reach = dz if h_up == 0 else dz - 1
            if reach == 0:
                continue
            h_down = 1 - h_up
            up[h_up][0]()
            add(half(reach, h_up), up[h_up][1])
            up[h_up] = put(reach, h_up)
            down[h_down][0]()
            add(half(-reach, h_down), down[h_down][1])
            down[h_down] = put(-reach, h_down)
            yield
    for h in (1, 0):
        up[h][0]()
        down[h][0]()
        add(sums.at[z, pl.ds(2 * h, 2)], up[h][1], down[h][1])


SUM_AB, SUM_C = 1536, 1024


def moe_part(
    post, norm_ref, ids_ref, gates_ref, out_ref,
    block_ab, block_c, g, gate_up, down, hidden, other, from_other, sums, other_c, from_c, sums_c,
    ring_a, ring_b, ring_c, ring_d, ring_z, row_in, block_in, z_in, final, loads, local_sem,
):
    z, y, x, c = here()
    lane = lax.broadcasted_iota(jnp.int32, (4, TABLE), 1)
    ids, gates = ids_ref[...], gates_ref[...].astype(F32)
    table = sum(jnp.where(ids[:, k : k + 1] == lane, gates[:, k : k + 1], 0.0) for k in range(ids.shape[1]))
    block_ab[...] = norm_ref[:, : Tokens.AB]
    block_c[:, : HALF - Tokens.AB] = norm_ref[:, Tokens.AB :]
    block_c[:, HALF - Tokens.AB :] = both_halves(table, c).astype(BF16)
    for _ in gather(post, (block_ab, block_c), Tokens(g), local_sem):
        pass
    for load in loads:
        load.wait()

    e = (y * NX + x) * 2 + c
    ours = (lax.broadcasted_iota(jnp.int32, (256, TABLE), 1) == e).astype(F32)

    def hidden_rows(i, carry):
        rows = [g[h, i].reshape(256, HALF + TABLE) for h in range(2)]
        weight = jnp.sum(
            (rows[0][:, HALF:].astype(F32) + rows[1][:, HALF:].astype(F32)) * ours, axis=1, keepdims=True
        )
        product = sum(
            lax.dot_general(
                rows[h][:, :HALF], gate_up[:, h * HALF : (h + 1) * HALF], (((1,), (1,)), ((), ())),
                preferred_element_type=F32,
            )
            for h in range(2)
        )
        gated, raised = product[:, :FFG], product[:, FFG:]
        hidden[i] = (gated / (1.0 + jnp.exp(-gated)) * raised * weight).astype(BF16).reshape(NX, 64, FFG)
        return carry

    lax.fori_loop(0, NY, hidden_rows, 0)

    xs = [step(x, o, NX) for o in range(NX)]
    ys = [step(y, o, NY) for o in range(NY)]
    tile = SUM_AB // 2
    twin = dev(z, y, x, 1 - c)

    def place(ref, name, o):
        if name == "a":
            return ref.at[ys[o], :, pl.ds(0, 32)]
        return ref.at[:, xs[o], pl.ds(32, 32)]

    def rows_of(name, o):
        return place(hidden, name, o)[...].reshape(128, FFG)

    def columns_c(i, rows):
        return jnp.dot(rows, down[i, :, SUM_AB:], preferred_element_type=F32).reshape(NX, NZ, 8, SUM_C)

    arrive = {}

    def give(name, o):
        rows = rows_of(name, o)
        for i in range(2):
            columns = pl.ds(i * tile, tile)
            part = jnp.dot(rows, down[1, :, columns], preferred_element_type=F32)
            place(other, name, o).at[:, :, columns][...] = part.reshape(4, 32, tile).astype(BF16)
        arrive[(name, o)] = post.put(place(other, name, o), place(from_other, name, o), twin, place(from_other, name, o))

    def take(name, o):
        arrive[(name, o)]()
        rows = rows_of(name, o)
        for i in range(2):
            columns = pl.ds(i * tile, tile)
            part = jnp.dot(rows, down[0, :, columns], preferred_element_type=F32).reshape(4, 32, tile)
            theirs = place(from_other, name, o).at[:, :, columns][...].astype(F32)
            place(sums, name, o).at[:, :, columns][...] = (part + theirs).astype(BF16)

    def give_c(i, carry):
        part = columns_c(1, hidden[i].reshape(256, FFG))
        for xx in range(NX):
            other_c[:, i, xx] = part[xx].astype(BF16)
        return carry

    def take_c(i, carry):
        part = columns_c(0, hidden[i].reshape(256, FFG))
        for xx in range(NX):
            sums_c[:, i, xx] = (part[xx] + from_c[:, i, xx].astype(F32)).astype(BF16)
        return carry

    a_lo, a_hi, b_lo, b_hi = [pl.ds(16 * i, 16) for i in range(4)]

    def to_x(s):
        return dev(z, y, step(x, s, NX), c)

    def to_y(s):
        return dev(z, step(y, s, NY), x, c)

    first = (
        Ring4(post, lambda p, r: sums.at[p, :, r], ring_a, y, a_lo, a_hi, to_y),
        Ring4(post, lambda p, r: sums.at[:, p, r], ring_b, x, b_lo, b_hi, to_x),
    )
    second = (
        Ring4(post, lambda p, r: sums.at[y, p, r], ring_c, x, a_lo, a_hi, to_x),
        Ring4(post, lambda p, r: sums.at[p, x, r], ring_d, y, b_lo, b_hi, to_y),
    )
    along_z = ring8(post, sums_c, ring_z, z, y, x, c)

    for o in (2, 1, 3):
        give("a", o)
        give("b", o)
    take("a", 2)
    take("b", 2)
    for ring in first:
        ring.far()
    lax.fori_loop(0, NY, give_c, 0)
    arrive_c = post.put(other_c, from_c, twin, from_c)
    for o in (1, 3):
        take("a", o)
        take("b", o)
    for ring in first:
        ring.near()
    give("a", 0)
    give("b", 0)
    arrive_c()
    lax.fori_loop(0, NY, take_c, 0)
    next(along_z)
    for ring in first:
        ring.last()
    take("a", 0)
    take("b", 0)
    next(along_z)
    next(along_z)
    for ring in first:
        ring.finish()
    for ring in second:
        ring.far()
        ring.near()
    next(along_z)
    for ring in second:
        ring.last()
    next(along_z)
    for ring in second:
        ring.finish()

    def zrows(at):
        return pl.ds(pl.multiple_of(at * 8, 8), 8)

    waits = [
        post.put(sums.at[y, x, zrows(step(z, j, NZ))], z_in.at[j], dev(step(z, j, NZ), y, x, c), z_in.at[j])
        for j in (1, 7, 2, 6, 3, 5, 4)
    ]
    keep = pltpu.make_async_copy(sums.at[y, x, zrows(z)], z_in.at[0], local_sem.at[0])
    keep.start()
    for _ in along_z:
        pass
    row_waits = [
        post.put(sums_c.at[z, step(y, o, NY)], row_in.at[o], to_y(o), row_in.at[o]) for o in (1, 3, 2)
    ]
    for wait in row_waits:
        wait()
    add(sums_c.at[z, y], *[row_in.at[o] for o in (1, 2, 3)])
    block_waits = [
        post.put(sums_c.at[z, y, step(x, o, NX)], block_in.at[o], to_x(o), block_in.at[o]) for o in (1, 3, 2)
    ]
    keep.wait()
    for wait in waits:
        wait()
    value = z_in[0].astype(F32)
    for j in range(1, NZ):
        value = value + z_in[j].astype(F32)
    final[c, :, :SUM_AB] = value
    for wait in block_waits:
        wait()
    value = sums_c[z, y, x].astype(F32)
    for o in range(1, 4):
        value = value + block_in[o].astype(F32)
    final[c, :, SUM_AB:] = value
    post.put(final.at[c], final.at[c], twin, final.at[1 - c])()
    own_rows(out_ref, final, c)


def layer_kernel(
    q_ref, own_ref, block_ab_ref, block_c_ref, own_bias_ref, ab_bias_ref, c_bias_ref,
    value_up_ref, hidden_ref, gain_ref, ids_ref, gates_ref, proj_hbm, gate_hbm, up_hbm, down_hbm,
    res_ref, out_ref,
    pool_ab, pool_c, top, total, acc, ctx,
    ctx_in, proj, p_other, p_from, parts, parts_in, full, residual, normed,
    block_ab, block_c, g, gate_up, down, hidden, other, from_other, sums, other_c, from_c, sums_c,
    ring_a, ring_b, ring_c, ring_d, ring_z, row_in, block_in, z_in, final,
    send, recv, local_sem, load_sem, ctx_send, ctx_recv, part_send, part_recv, sib_send, sib_recv,
):
    z, y, x, c = here()
    devices = 2 * NX * NY
    e = (y * NX + x) * 2 + c

    def column_half(half):
        return pl.ds(pl.multiple_of(half * HALF, 128), HALF)

    pairs = [(proj_hbm.at[:, column_half(half)], proj.at[i]) for i, half in enumerate((c, 1 - c))]
    pairs += [(gate_hbm.at[0], gate_up.at[pl.ds(0, FFG)]), (up_hbm.at[0], gate_up.at[pl.ds(FFG, FFG)])]
    pairs += [(down_hbm.at[0, :, column_half(half)], down.at[i]) for i, half in enumerate((c, 1 - c))]
    loads = [pltpu.make_async_copy(src, dst, load_sem.at[i]) for i, (src, dst) in enumerate(pairs)]
    for load in loads:
        load.start()

    barrier = pltpu.get_barrier_semaphore()

    def hello(j, carry):
        pl.semaphore_signal(
            barrier, inc=1, device_id=(z, lax.rem(e + j, devices)), device_id_type=MESH
        )
        return carry

    lax.fori_loop(1, devices, hello, 0)
    for j in range(1, NZ):
        pl.semaphore_signal(barrier, inc=1, device_id=dev(step(z, j, NZ), y, x, c), device_id_type=MESH)
    pl.semaphore_wait(barrier, devices - 1 + NZ - 1)

    post = Post(send, recv)
    attend_part(
        post, q_ref, own_ref, block_ab_ref, block_c_ref, own_bias_ref, ab_bias_ref, c_bias_ref, ctx,
        pool_ab, pool_c, top, total, acc, local_sem,
    )
    finish = project_part(
        ctx, value_up_ref, hidden_ref, gain_ref, normed,
        ctx_in, proj, p_other, p_from, parts, parts_in, full, residual, loads[:2],
        local_sem.at[0], ctx_send, ctx_recv, part_send, part_recv, sib_send, sib_recv,
    )
    moe_part(
        post, normed, ids_ref, gates_ref, out_ref,
        block_ab, block_c, g, gate_up, down, hidden, other, from_other, sums, other_c, from_c, sums_c,
        ring_a, ring_b, ring_c, ring_d, ring_z, row_in, block_in, z_in, final, loads[2:], local_sem,
    )
    own_rows(res_ref, residual, c)
    finish()
    post.drain()


def layer(*operands):
    vmem = pl.BlockSpec(memory_space=pltpu.VMEM)
    hbm = pl.BlockSpec(memory_space=pl.ANY)
    chips, rows = NX * NY, 256
    return pl.pallas_call(
        layer_kernel,
        out_shape=(jax.ShapeDtypeStruct((4, D), F32), jax.ShapeDtypeStruct((4, D), F32)),
        in_specs=[vmem] * 12 + [hbm] * 4,
        out_specs=(vmem, vmem),
        scratch_shapes=[
            pltpu.VMEM((2, NY, NX, NZ, Pool.AB, KPAD), BF16),
            pltpu.VMEM((2, NZ, Pool.C, KPAD), BF16),
            pltpu.VMEM((rows, 1), F32),
            pltpu.VMEM((rows, 1), F32),
            pltpu.VMEM((rows, LAT), F32),
            pltpu.VMEM((2 * chips, 8, LAT), BF16),
            pltpu.VMEM((2 * chips, 8, LAT), BF16),
            pltpu.VMEM((2, 256, HALF), BF16),
            pltpu.VMEM((chips, 8, HALF), BF16),
            pltpu.VMEM((chips, 8, HALF), BF16),
            pltpu.VMEM((chips, 8, HALF), BF16),
            pltpu.VMEM((chips, 8, HALF), BF16),
            pltpu.VMEM((chips, 8, HALF), F32),
            pltpu.VMEM((2, 8, HALF), F32),
            pltpu.VMEM((8, HALF), BF16),
            pltpu.VMEM((8, Tokens.AB), BF16),
            pltpu.VMEM((8, Tokens.C), BF16),
            pltpu.VMEM((2, NY, NX, NZ * 8, HALF + TABLE), BF16),
            pltpu.VMEM((2 * FFG, D), BF16),
            pltpu.VMEM((2, FFG, HALF), BF16),
            pltpu.VMEM((NY, NX, 64, FFG), BF16),
            pltpu.VMEM((NY, NX, 64, SUM_AB), BF16),
            pltpu.VMEM((NY, NX, 64, SUM_AB), BF16),
            pltpu.VMEM((NY, NX, 64, SUM_AB), BF16),
            pltpu.VMEM((NZ, NY, NX, 8, SUM_C), BF16),
            pltpu.VMEM((NZ, NY, NX, 8, SUM_C), BF16),
            pltpu.VMEM((NZ, NY, NX, 8, SUM_C), BF16),
            pltpu.VMEM((6, NX, 16, SUM_AB), BF16),
            pltpu.VMEM((6, NY, 16, SUM_AB), BF16),
            pltpu.VMEM((6, 16, SUM_AB), BF16),
            pltpu.VMEM((6, 16, SUM_AB), BF16),
            pltpu.VMEM((14, NY // 2, NX, 8, SUM_C), BF16),
            pltpu.VMEM((4, NX, 8, SUM_C), BF16),
            pltpu.VMEM((4, 8, SUM_C), BF16),
            pltpu.VMEM((NZ, 8, SUM_AB), BF16),
            pltpu.VMEM((2, 8, HALF), F32),
            pltpu.SemaphoreType.DMA((COPIES,)),
            pltpu.SemaphoreType.DMA((COPIES,)),
            pltpu.SemaphoreType.DMA((2,)),
            pltpu.SemaphoreType.DMA((6,)),
            pltpu.SemaphoreType.DMA((2 * chips,)),
            pltpu.SemaphoreType.DMA((2 * chips,)),
            pltpu.SemaphoreType.DMA((chips,)),
            pltpu.SemaphoreType.DMA((chips,)),
            pltpu.SemaphoreType.DMA((2,)),
            pltpu.SemaphoreType.DMA((2,)),
        ],
        compiler_params=pltpu.CompilerParams(
            collective_id=0, has_side_effects=True, vmem_limit_bytes=60 * 2**20
        ),
        name="layer",
    )(*operands)


def per_device(
    hidden_in, query, prefix_pool, suffix_cache, block_list, prefix_count, suffix_count, value_up,
    out_proj, norm_gain, expert_ids, gate_weights, gate_proj, up_proj, down_proj,
):
    e = lax.axis_index("expert")
    core, chip = lax.rem(e, 2), lax.div(e, 2)

    def padded(v):
        return jnp.pad(v, ((0, 0), (0, KPAD - KDIM)))

    block_ab = lax.dynamic_slice(prefix_pool, (chip, core * (24 * KDIM)), (1, 24 * KDIM))
    block_ab = padded(block_ab.reshape(24, KDIM))[None]
    block_c = lax.dynamic_slice(prefix_pool, (core * 8, 48 * KDIM), (8, 16 * KDIM))
    block_c = padded(block_c.reshape(128, KDIM))
    q = query.reshape(4, 32, 2, KDIM).transpose(1, 2, 0, 3).reshape(256, KDIM)
    q = jnp.pad(q, ((0, 0), (0, KPAD - KDIM)))
    own = jnp.pad(suffix_cache.reshape(4 * SUFFIX, KDIM), ((0, 0), (0, KPAD - KDIM)))
    in_prefix = jnp.arange(32, dtype=jnp.int32)[None, :] < prefix_count[:, None]
    listed = jnp.where(in_prefix, block_list, -1)
    member = jnp.any(listed[:, :, None] == jnp.arange(128, dtype=jnp.int32), axis=1)
    member = member.reshape(4, NZ, 16).transpose(2, 0, 1)
    member = jnp.where(member, 0.0, NEG_FILL).astype(F32)
    ab_bias = jnp.broadcast_to(
        member[:, None, :, None, :, None], (16, 2, 4, 2, NZ, Pool.AB)
    ).reshape(16, 8, 2 * NZ * Pool.AB)
    c_bias = jnp.broadcast_to(
        member.transpose(2, 1, 0)[:, None, :, :, None], (NZ, 2, 4, 16, 16)
    ).reshape(NZ, 8, 2 * Pool.C)
    row = jnp.arange(4 * SUFFIX, dtype=jnp.int32)
    own_live = (row // SUFFIX == jnp.arange(4, dtype=jnp.int32)[:, None]) & (
        row % SUFFIX < suffix_count[:, None]
    )
    own_live = jnp.concatenate([own_live, own_live], axis=0)
    own_bias = jnp.where(own_live, 0.0, NEG_FILL).astype(F32)
    return layer(
        q, own, block_ab, block_c, own_bias, ab_bias, c_bias,
        value_up, hidden_in, norm_gain.reshape(2, 1, HALF), expert_ids, gate_weights,
        out_proj, gate_proj.transpose(0, 2, 1), up_proj.transpose(0, 2, 1), down_proj,
    )


def solution(mesh):
    rows = P(("dp", "expert"), None)
    in_specs = (
        rows, rows, P("dp", None), rows, rows, P(("dp", "expert")), P(("dp", "expert")),
        P("expert", None, None), P("expert", None), P(), rows, rows,
        P("expert", None, "dp"), P("expert", None, "dp"), P("expert", "dp", None),
    )
    return jax.shard_map(
        per_device, mesh=mesh, in_specs=in_specs, out_specs=(rows, rows), check_vma=False
    )
```

time: 214 us -> 185 us (0.86)
  Pallas kernels: 190 us -> 170 us
  local copies, waits for them, and re-layouts: 16.5 us -> 12.3 us
  other arithmetic: 6.14 us -> 2.2 us
    pallas_call x3 -> x1, Pallas kernels: 190 us -> 170 us  [layer(): pl.pallas_call(layer_kernel, out_shape=(jax.ShapeDtypeStruct((4, D), F32)...]
    unnamed x12 -> x10, local copies, waits for them, and re-layouts: 9.14 us -> 4.32 us
    reshape x3 -> x5, local copies, waits for them, and re-layouts: 0.69 us -> 2.87 us  [the longest x1 1.14 us: per_device(): ab_bias = jnp.broadcast_to(member[:, None, :, None, :, None], (16, 2, 4,...]
where the time goes in v2:
time: 185 us
  Pallas kernels  170 us (92%)
  local copies, waits for them, and re-layouts  12.3 us (7%)
  other arithmetic  2.2 us (1%)
    pallas_call x1, Pallas kernels, layer(): pl.pallas_call(layer_kernel, out_shape=(jax.ShapeDtypeStruct((4, D), F32)...  170 us
    unnamed x10, local copies, waits for them, and re-layouts  4.32 us

profile of v2, /device:TPU:1, one launch (start us, length us, event | category | flops | bytes accessed | tf_op | source)
XLA Modules:
  0.0 184.8 jit_solution(3784210106981166969)
XLA Ops:
  0.7 1.2 copy-done
  1.9 0.2 dynamic-slice_reduce_fusion
  2.1 0.1 reshape.65
  2.2 0.6 pad_bitcast_fusion.block_ab_ref
  2.9 0.2 reshape.66
  3.0 0.7 pad.19.block_c_ref
  3.7 0.7 fusion.1
  4.5 0.6 add_select_fusion.own_bias_ref
  5.1 0.8 fusion.9
  5.8 0.1 fusion
  6.1 0.1 broadcast_in_dim.49
  6.2 1.1 reshape.67.ab_bias_ref
  7.4 0.1 broadcast_in_dim.50
  7.5 0.9 reshape.68.c_bias_ref
  8.4 0.4 reshape.62
  8.8 0.3 copy.28
  9.1 0.2 reshape.63
  9.2 0.8 pad.16.q_ref
  10.0 0.7 reshape.64
  10.7 0.9 pad.17.own_ref
  11.6 0.6 reshape.70.gain_ref
  12.2 169.6 %layer.1 = (f32[4,5120]{1,0:T(4,128)}, f32[4,5120]{1,0:T(4,128)}) custom-call(bf16[256,640]{1,0:T(8,128)(2,1)} %pad.16.q_ref, bf16[512,640]{1,0:T(8,128)(2,1)} %pad.17.own_ref, bf16[1,24,640]{2,1,0:T(8,128)(2,1)} %pad_bitcast_fusion.block_ab_ref, bf16[128,640]{1,0:T(8,128)(2,1)} %pad.19.block_c_ref, f32[8,512]{1,0:T(8,128)} %add_select_fusion.own_bias_ref, ...), custom_call_target="tpu_custom_call" | custom-call | tf_op jit(solution)/shard_map/layer/pallas_call | solution.py:794
  181.8 1.5 copy.31
  183.3 1.5 copy.32
  (13 shorter events, 0.2 us)
Async XLA Ops:
  0.6 1.3 copy-start
  3.0 5.4 %copy-start.2 = (bf16[4,36864]{1,0:T(4,128)(2,1)S(1)}, bf16[4,36864]{1,0:T(4,128)(2,1)}, u32[]{:S(2)}) copy-start(bf16[4,36864]{1,0:T(4,128)(2,1)} %param.16) | copy-start | bytes 884740
  7.4 2.6 %copy-start.1 = (bf16[4,73728]{1,0:T(4,128)(2,1)S(1)}, bf16[4,73728]{1,0:T(4,128)(2,1)}, u32[]{:S(2)}) copy-start(bf16[4,73728]{1,0:T(4,128)(2,1)} %param.18) | copy-start | bytes 1769476
  9.1 2.5 %copy-start.3 = (bf16[5120]{0:T(1024)(128)(2,1)S(1)}, bf16[5120]{0:T(1024)(128)(2,1)}, u32[]{:S(2)}) copy-start(bf16[5120]{0:T(1024)(128)(2,1)} %param.24) | copy-start | bytes 30724

commit v3 on v2

--- a/solution.py
+++ b/solution.py
@@ -11,7 +11,6 @@
 BLOCK = 64
 SUFFIX = 128
 KDIM = 576
-KPAD = 640
 D = 5120
 HALF = 2560
 FFG = 192
@@ -20,6 +19,7 @@
 NEG_FILL = -1e30
 SCORE_SCALE = 192.0 ** (-0.5)
 NORM_EPS = 1e-06
+LOG2_E = 1.4426950408889634
 
 NX, NY, NZ = 4, 4, 8
 MESH = pl.DeviceIdType.MESH
@@ -298,25 +298,63 @@
 
 
 def attend_part(
-    post, q_ref, own_ref, block_ab_ref, block_c_ref, own_bias_ref, ab_bias_ref, c_bias_ref, out_ref,
+    post, q_ref, own_ref, block_ab_ref, block_c_ref, list_ref, prefix_ref, suffix_ref, out_ref,
     g_ab, g_c, top, total, acc, local_sem,
 ):
+    def request(shape):
+        return lax.rem(lax.broadcasted_iota(jnp.int32, shape, 0), 4)
+
+    def by_request(ref, shape):
+        turn = request(shape)
+        return jnp.where(turn == 0, ref[0], jnp.where(turn == 1, ref[1], jnp.where(turn == 2, ref[2], ref[3])))
+
+    def live_bias(live):
+        return (live.astype(F32) - 1.0) * -NEG_FILL
+
+    def member_blocks():
+        listed = jnp.concatenate([list_ref[...], list_ref[...]], axis=0)
+        block, count = lax.broadcasted_iota(jnp.int32, (8, 128), 1), by_request(prefix_ref, (8, 128))
+        member = jnp.zeros((8, 128), F32)
+        for j in range(listed.shape[1]):
+            member = jnp.where((listed[:, j : j + 1] == block) & (j < count), 1.0, member)
+        return member.astype(BF16)
+
+    def own_bias():
+        shape = (8, 4 * SUFFIX)
+        row = lax.broadcasted_iota(jnp.int32, shape, 1)
+        place = row - SUFFIX * request(shape)
+        return live_bias(jnp.where((place >= 0) & (place < by_request(suffix_ref, shape)), 1.0, 0.0))
+
+    def pool_bias(member, block_of_key):
+        block = lax.broadcasted_iota(jnp.int32, block_of_key.shape, 0)
+        spread = jnp.where(block == block_of_key, 1.0, 0.0).astype(BF16)
+        return live_bias(jnp.dot(member, spread, preferred_element_type=F32))
+
+    def ab_bias(member, k):
+        key = lax.broadcasted_iota(jnp.int32, (128, 2 * NZ * Pool.AB), 1)
+        zz = sum((key >= Pool.AB * i).astype(jnp.int32) for i in range(1, 2 * NZ))
+        return pool_bias(member, (zz - jnp.where(zz >= NZ, NZ, 0)) * 16 + k)
+
+    def c_bias(member, zz):
+        key = lax.broadcasted_iota(jnp.int32, (128, 2 * Pool.C), 1)
+        return pool_bias(member, lax.shift_right_logical(key, 4) + zz * 16)
+
     def merge(keys, bias, first=False):
         q = q_ref[...]
         scores = lax.dot_general(q, keys, (((1,), (1,)), ((), ())), preferred_element_type=F32)
         rows, width = scores.shape
-        scores = (scores.reshape(rows // 8, 8, width) * SCORE_SCALE + bias[None]).reshape(rows, width)
+        scores = (scores.reshape(rows // 8, 8, width) * (SCORE_SCALE * LOG2_E) + bias[None]).reshape(rows, width)
         best = jnp.max(scores, axis=1, keepdims=True)
         if not first:
             best = jnp.maximum(best, top[...])
-        weights = jnp.exp(scores - best)
+        weights = jnp.exp2(scores - best)
         summed = jnp.sum(weights, axis=1, keepdims=True)
         mixed = jnp.dot(weights.astype(BF16), keys[:, :LAT], preferred_element_type=F32)
         if first:
             total[...] = summed
             acc[...] = mixed
         else:
-            scale = jnp.exp(top[...] - best)
+            scale = jnp.exp2(top[...] - best)
             total[...] = total[...] * scale + summed
             acc[...] = acc[...] * scale + mixed
         top[...] = best
@@ -326,16 +364,17 @@
     started = False
     for parts in gather(post, block, pool, local_sem):
         if not started:
-            merge(own_ref[...], own_bias_ref[...], first=True)
+            merge(own_ref[...], own_bias(), first=True)
+            member = member_blocks()
             started = True
         for part in parts:
             if len(part) == 2:
                 yy, xx = part
-                keys = jnp.concatenate([g_ab[h, yy, xx].reshape(NZ * Pool.AB, KPAD) for h in range(2)], axis=0)
-                merge(keys, ab_bias_ref[yy * NX + xx])
+                keys = jnp.concatenate([g_ab[h, yy, xx].reshape(NZ * Pool.AB, KDIM) for h in range(2)], axis=0)
+                merge(keys, ab_bias(member, yy * NX + xx))
             else:
                 keys = jnp.concatenate([g_c[0, part[0]], g_c[1, part[0]]], axis=0)
-                merge(keys, c_bias_ref[part[0]])
+                merge(keys, c_bias(member, part[0]))
     out_ref[...] = (acc[...] / total[...]).reshape(out_ref.shape).astype(BF16)
 
 
@@ -457,7 +496,7 @@
     swap_in.wait_recv()
     squares = sum(jnp.sum(res_ref[h] * res_ref[h], axis=1, keepdims=True) for h in range(2))
     scale = lax.rsqrt(squares * (1.0 / D) + NORM_EPS)
-    norm_ref[...] = (res_ref[c] * scale * gain_ref[c].astype(F32)).astype(BF16)
+    norm_ref[...] = (res_ref[c] * scale * gain_ref[c]).astype(BF16)
 
     def finish():
         swap_copy.wait_send()
@@ -656,15 +695,21 @@
     )
     along_z = ring8(post, sums_c, ring_z, z, y, x, c)
 
-    for o in (2, 1, 3):
-        give("a", o)
-        give("b", o)
+    lax.fori_loop(0, NY, give_c, 0)
+    arrive_c = post.put(other_c, from_c, twin, from_c)
+    give("a", 2)
+    give("b", 2)
+    arrive_c()
+    lax.fori_loop(0, NY, take_c, 0)
+    next(along_z)
     take("a", 2)
     take("b", 2)
     for ring in first:
         ring.far()
-    lax.fori_loop(0, NY, give_c, 0)
-    arrive_c = post.put(other_c, from_c, twin, from_c)
+    for o in (1, 3):
+        give("a", o)
+        give("b", o)
+    next(along_z)
     for o in (1, 3):
         take("a", o)
         take("b", o)
@@ -672,14 +717,11 @@
         ring.near()
     give("a", 0)
     give("b", 0)
-    arrive_c()
-    lax.fori_loop(0, NY, take_c, 0)
     next(along_z)
     for ring in first:
         ring.last()
     take("a", 0)
     take("b", 0)
-    next(along_z)
     next(along_z)
     for ring in first:
         ring.finish()
@@ -731,7 +773,7 @@
 
 
 def layer_kernel(
-    q_ref, own_ref, block_ab_ref, block_c_ref, own_bias_ref, ab_bias_ref, c_bias_ref,
+    q_ref, own_ref, block_ab_ref, block_c_ref, list_ref, prefix_ref, suffix_ref,
     value_up_ref, hidden_ref, gain_ref, ids_ref, gates_ref, proj_hbm, gate_hbm, up_hbm, down_hbm,
     res_ref, out_ref,
     pool_ab, pool_c, top, total, acc, ctx,
@@ -769,7 +811,7 @@
 
     post = Post(send, recv)
     attend_part(
-        post, q_ref, own_ref, block_ab_ref, block_c_ref, own_bias_ref, ab_bias_ref, c_bias_ref, ctx,
+        post, q_ref, own_ref, block_ab_ref, block_c_ref, list_ref, prefix_ref, suffix_ref, ctx,
         pool_ab, pool_c, top, total, acc, local_sem,
     )
     finish = project_part(
@@ -794,11 +836,11 @@
     return pl.pallas_call(
         layer_kernel,
         out_shape=(jax.ShapeDtypeStruct((4, D), F32), jax.ShapeDtypeStruct((4, D), F32)),
-        in_specs=[vmem] * 12 + [hbm] * 4,
+        in_specs=[vmem] * 5 + [pl.BlockSpec(memory_space=pltpu.SMEM)] * 2 + [vmem] * 5 + [hbm] * 4,
         out_specs=(vmem, vmem),
         scratch_shapes=[
-            pltpu.VMEM((2, NY, NX, NZ, Pool.AB, KPAD), BF16),
-            pltpu.VMEM((2, NZ, Pool.C, KPAD), BF16),
+            pltpu.VMEM((2, NY, NX, NZ, Pool.AB, KDIM), BF16),
+            pltpu.VMEM((2, NZ, Pool.C, KDIM), BF16),
             pltpu.VMEM((rows, 1), F32),
             pltpu.VMEM((rows, 1), F32),
             pltpu.VMEM((rows, LAT), F32),
@@ -858,36 +900,13 @@
     e = lax.axis_index("expert")
     core, chip = lax.rem(e, 2), lax.div(e, 2)
 
-    def padded(v):
-        return jnp.pad(v, ((0, 0), (0, KPAD - KDIM)))
-
-    block_ab = lax.dynamic_slice(prefix_pool, (chip, core * (24 * KDIM)), (1, 24 * KDIM))
-    block_ab = padded(block_ab.reshape(24, KDIM))[None]
-    block_c = lax.dynamic_slice(prefix_pool, (core * 8, 48 * KDIM), (8, 16 * KDIM))
-    block_c = padded(block_c.reshape(128, KDIM))
+    block_ab = lax.dynamic_slice(prefix_pool, (chip, core * (24 * KDIM)), (1, 24 * KDIM)).reshape(1, 24, KDIM)
+    block_c = lax.dynamic_slice(prefix_pool, (core * 8, 48 * KDIM), (8, 16 * KDIM)).reshape(128, KDIM)
     q = query.reshape(4, 32, 2, KDIM).transpose(1, 2, 0, 3).reshape(256, KDIM)
-    q = jnp.pad(q, ((0, 0), (0, KPAD - KDIM)))
-    own = jnp.pad(suffix_cache.reshape(4 * SUFFIX, KDIM), ((0, 0), (0, KPAD - KDIM)))
-    in_prefix = jnp.arange(32, dtype=jnp.int32)[None, :] < prefix_count[:, None]
-    listed = jnp.where(in_prefix, block_list, -1)
-    member = jnp.any(listed[:, :, None] == jnp.arange(128, dtype=jnp.int32), axis=1)
-    member = member.reshape(4, NZ, 16).transpose(2, 0, 1)
-    member = jnp.where(member, 0.0, NEG_FILL).astype(F32)
-    ab_bias = jnp.broadcast_to(
-        member[:, None, :, None, :, None], (16, 2, 4, 2, NZ, Pool.AB)
-    ).reshape(16, 8, 2 * NZ * Pool.AB)
-    c_bias = jnp.broadcast_to(
-        member.transpose(2, 1, 0)[:, None, :, :, None], (NZ, 2, 4, 16, 16)
-    ).reshape(NZ, 8, 2 * Pool.C)
-    row = jnp.arange(4 * SUFFIX, dtype=jnp.int32)
-    own_live = (row // SUFFIX == jnp.arange(4, dtype=jnp.int32)[:, None]) & (
-        row % SUFFIX < suffix_count[:, None]
-    )
-    own_live = jnp.concatenate([own_live, own_live], axis=0)
-    own_bias = jnp.where(own_live, 0.0, NEG_FILL).astype(F32)
+    own = suffix_cache.reshape(4 * SUFFIX, KDIM)
     return layer(
-        q, own, block_ab, block_c, own_bias, ab_bias, c_bias,
-        value_up, hidden_in, norm_gain.reshape(2, 1, HALF), expert_ids, gate_weights,
+        q, own, block_ab, block_c, block_list, prefix_count, suffix_count,
+        value_up, hidden_in, norm_gain.astype(F32).reshape(2, 1, HALF), expert_ids, gate_weights,
         out_proj, gate_proj.transpose(0, 2, 1), up_proj.transpose(0, 2, 1), down_proj,
     )
 

time: 185 us -> 177 us (0.957)
  Pallas kernels: 170 us -> 166 us
  local copies, waits for them, and re-layouts: 12.3 us -> 8.88 us
    pallas_call x1, Pallas kernels: 170 us -> 166 us  [layer(): pl.pallas_call(layer_kernel, out_shape=(jax.ShapeDtypeStruct((4, D), F32)...]
    pad x3 -> x0, local copies, waits for them, and re-layouts: 2.35 us -> none  [the longest x1 0.91 us: per_device(): jnp.pad(suffix_cache.reshape(4 * SUFFIX, KDIM), ((0, 0), (0, KPAD - KDIM)))]
    unnamed x10 -> x6, local copies, waits for them, and re-layouts: 4.32 us -> 3.07 us
where the time goes in v3:
time: 177 us
  Pallas kernels  166 us (94%)
  local copies, waits for them, and re-layouts  8.88 us (5%)
    pallas_call x1, Pallas kernels, layer(): pl.pallas_call(layer_kernel, out_shape=(jax.ShapeDtypeStruct((4, D), F32)...  166 us

profile of v3, /device:TPU:1, one launch (start us, length us, event | category | flops | bytes accessed | tf_op | source)
XLA Modules:
  0.0 176.7 jit_solution(7117458228456690046)
XLA Ops:
  0.6 0.0 copy-start
  0.6 0.0 copy-start.1
  0.7 1.4 reshape.31
  2.1 0.0 copy-done
  2.1 0.2 dynamic-slice_reduce_fusion
  2.3 0.7 reshape.27.block_ab_ref
  3.1 0.8 reshape.28.block_c_ref
  3.9 1.4 reshape.24
  5.3 0.3 copy.20
  5.5 0.9 reshape.25.q_ref
  6.4 0.0 copy-done.1
  6.4 1.5 reshape.26.own_ref
  7.9 165.7 %layer.1 = (f32[4,5120]{1,0:T(4,128)}, f32[4,5120]{1,0:T(4,128)}) custom-call(bf16[256,576]{1,0:T(8,128)(2,1)} %reshape.25.q_ref, bf16[512,576]{1,0:T(8,128)(2,1)} %reshape.26.own_ref, bf16[1,24,576]{2,1,0:T(8,128)(2,1)} %reshape.27.block_ab_ref, bf16[128,576]{1,0:T(8,128)(2,1)} %reshape.28.block_c_ref, s32[4,32]{1,0:T(4,128)} %list_ref.1, s32[4]{0:T(128)} %prefix_ref.1, ...), custom_call_target="tpu_custom_call" | custom-call | tf_op jit(solution)/shard_map/layer/pallas_call | solution.py:836
  173.6 1.5 copy.23
  175.2 1.5 copy.24
  (1 shorter events, 0.0 us)
Async XLA Ops:
  0.6 1.5 copy-start
  0.6 5.8 %copy-start.1 = (bf16[4,73728]{1,0:T(4,128)(2,1)S(1)}, bf16[4,73728]{1,0:T(4,128)(2,1)}, u32[]{:S(2)}) copy-start(bf16[4,73728]{1,0:T(4,128)(2,1)} %param.18) | copy-start | bytes 1769476

commit v4 on v3

--- a/solution.py
+++ b/solution.py
@@ -275,7 +275,7 @@
 
 
 class Tokens:
-    AB, C = 1664, 1024
+    AB, C = 1792, 896
 
     def __init__(self, g):
         self.g = g
@@ -326,17 +326,17 @@
         return live_bias(jnp.where((place >= 0) & (place < by_request(suffix_ref, shape)), 1.0, 0.0))
 
     def pool_bias(member, block_of_key):
-        block = lax.broadcasted_iota(jnp.int32, block_of_key.shape, 0)
+        block = lax.broadcasted_iota(jnp.int32, (128, block_of_key.shape[1]), 0)
         spread = jnp.where(block == block_of_key, 1.0, 0.0).astype(BF16)
         return live_bias(jnp.dot(member, spread, preferred_element_type=F32))
 
     def ab_bias(member, k):
-        key = lax.broadcasted_iota(jnp.int32, (128, 2 * NZ * Pool.AB), 1)
+        key = lax.broadcasted_iota(jnp.int32, (1, 2 * NZ * Pool.AB), 1)
         zz = sum((key >= Pool.AB * i).astype(jnp.int32) for i in range(1, 2 * NZ))
         return pool_bias(member, (zz - jnp.where(zz >= NZ, NZ, 0)) * 16 + k)
 
     def c_bias(member, zz):
-        key = lax.broadcasted_iota(jnp.int32, (128, 2 * Pool.C), 1)
+        key = lax.broadcasted_iota(jnp.int32, (1, 2 * Pool.C), 1)
         return pool_bias(member, lax.shift_right_logical(key, 4) + zz * 16)
 
     def merge(keys, bias, first=False):
@@ -462,13 +462,6 @@
         full[:, :, columns] = part.reshape(chips, 8, tile)
     sib.wait()
 
-    def total(j, carry):
-        full[j] = full[j] + from_other[j].astype(F32)
-        parts[j] = full[j].astype(BF16)
-        return carry
-
-    lax.fori_loop(0, chips, total, 0)
-
     def part_copy(j):
         to = lax.rem(chip + j, chips)
         return pltpu.make_async_remote_copy(
@@ -476,7 +469,13 @@
             device_id=(z, to * 2 + c), device_id_type=MESH,
         )
 
-    each(1, chips, lambda j: part_copy(j).start())
+    def give_part(j):
+        to = lax.rem(chip + j, chips)
+        parts[to] = (full[to] + from_other[to].astype(F32)).astype(BF16)
+        part_copy(j).start()
+
+    each(1, chips, give_part)
+    full[chip] = full[chip] + from_other[chip].astype(F32)
     res_ref[c] = full[chip] + hidden_own
     each(1, chips, lambda j: part_copy(j).wait_recv())
 
@@ -589,13 +588,13 @@
         add(sums.at[z, pl.ds(2 * h, 2)], up[h][1], down[h][1])
 
 
-SUM_AB, SUM_C = 1536, 1024
+SUM_AB, SUM_C = 1792, 768
 
 
 def moe_part(
     post, norm_ref, ids_ref, gates_ref, out_ref,
     block_ab, block_c, g, gate_up, down, hidden, other, from_other, sums, other_c, from_c, sums_c,
-    ring_a, ring_b, ring_c, ring_d, ring_z, row_in, block_in, z_in, final, loads, local_sem,
+    ring_a, ring_b, ring_c, ring_d, ring_z, row_in, block_in, z_in, final, product_ab, loads, local_sem,
 ):
     z, y, x, c = here()
     lane = lax.broadcasted_iota(jnp.int32, (4, TABLE), 1)
@@ -604,26 +603,40 @@
     block_ab[...] = norm_ref[:, : Tokens.AB]
     block_c[:, : HALF - Tokens.AB] = norm_ref[:, Tokens.AB :]
     block_c[:, HALF - Tokens.AB :] = both_halves(table, c).astype(BF16)
-    for _ in gather(post, (block_ab, block_c), Tokens(g), local_sem):
-        pass
-    for load in loads:
-        load.wait()
+    columns_ab = [pl.ds(h * HALF, Tokens.AB) for h in range(2)]
+    columns_rest = [pl.ds(h * HALF + Tokens.AB, HALF - Tokens.AB) for h in range(2)]
+
+    def times(rows, columns):
+        return lax.dot_general(rows, gate_up[:, columns], (((1,), (1,)), ((), ())), preferred_element_type=F32)
+
+    chunks = []
+    for parts in gather(post, (block_ab, block_c), Tokens(g), local_sem):
+        chunks += [part for part in parts if len(part) == 2]
+        if len(chunks) == 4:
+            if loads:
+                for load in loads:
+                    load.wait()
+                loads = []
+            part = sum(
+                times(jnp.concatenate([g[h, yy, xx, :, : Tokens.AB] for yy, xx in chunks], axis=0), columns_ab[h])
+                for h in range(2)
+            )
+            for i, (yy, xx) in enumerate(chunks):
+                product_ab[yy, xx] = part[i * 64 : (i + 1) * 64]
+            chunks = []
 
     e = (y * NX + x) * 2 + c
     ours = (lax.broadcasted_iota(jnp.int32, (256, TABLE), 1) == e).astype(F32)
 
     def hidden_rows(i, carry):
-        rows = [g[h, i].reshape(256, HALF + TABLE) for h in range(2)]
+        rows = [g[h, i, :, :, Tokens.AB :].reshape(256, Tokens.C) for h in range(2)]
+        rest = HALF - Tokens.AB
         weight = jnp.sum(
-            (rows[0][:, HALF:].astype(F32) + rows[1][:, HALF:].astype(F32)) * ours, axis=1, keepdims=True
+            (rows[0][:, rest:].astype(F32) + rows[1][:, rest:].astype(F32)) * ours, axis=1, keepdims=True
         )
-        product = sum(
-            lax.dot_general(
-                rows[h][:, :HALF], gate_up[:, h * HALF : (h + 1) * HALF], (((1,), (1,)), ((), ())),
-                preferred_element_type=F32,
-            )
-            for h in range(2)
-        )
+        product = product_ab[i].reshape(256, 2 * FFG)
+        for h in range(2):
+            product = product + times(rows[h][:, :rest], columns_rest[h])
         gated, raised = product[:, :FFG], product[:, FFG:]
         hidden[i] = (gated / (1.0 + jnp.exp(-gated)) * raised * weight).astype(BF16).reshape(NX, 64, FFG)
         return carry
@@ -779,7 +792,7 @@
     pool_ab, pool_c, top, total, acc, ctx,
     ctx_in, proj, p_other, p_from, parts, parts_in, full, residual, normed,
     block_ab, block_c, g, gate_up, down, hidden, other, from_other, sums, other_c, from_c, sums_c,
-    ring_a, ring_b, ring_c, ring_d, ring_z, row_in, block_in, z_in, final,
+    ring_a, ring_b, ring_c, ring_d, ring_z, row_in, block_in, z_in, final, product_ab,
     send, recv, local_sem, load_sem, ctx_send, ctx_recv, part_send, part_recv, sib_send, sib_recv,
 ):
     z, y, x, c = here()
@@ -822,7 +835,7 @@
     moe_part(
         post, normed, ids_ref, gates_ref, out_ref,
         block_ab, block_c, g, gate_up, down, hidden, other, from_other, sums, other_c, from_c, sums_c,
-        ring_a, ring_b, ring_c, ring_d, ring_z, row_in, block_in, z_in, final, loads[2:], local_sem,
+        ring_a, ring_b, ring_c, ring_d, ring_z, row_in, block_in, z_in, final, product_ab, loads[2:], local_sem,
     )
     own_rows(res_ref, residual, c)
     finish()
@@ -875,6 +888,7 @@
             pltpu.VMEM((4, 8, SUM_C), BF16),
             pltpu.VMEM((NZ, 8, SUM_AB), BF16),
             pltpu.VMEM((2, 8, HALF), F32),
+            pltpu.VMEM((NY, NX, 64, 2 * FFG), F32),
             pltpu.SemaphoreType.DMA((COPIES,)),
             pltpu.SemaphoreType.DMA((COPIES,)),
             pltpu.SemaphoreType.DMA((2,)),

time: 177 us -> 173 us (0.977)
  Pallas kernels: 166 us -> 162 us
    pallas_call x1, Pallas kernels: 166 us -> 162 us  [layer(): pl.pallas_call(layer_kernel, out_shape=(jax.ShapeDtypeStruct((4, D), F32)...]
where the time goes in v4:
time: 173 us
  Pallas kernels  162 us (94%)
  local copies, waits for them, and re-layouts  8.88 us (5%)
    pallas_call x1, Pallas kernels, layer(): pl.pallas_call(layer_kernel, out_shape=(jax.ShapeDtypeStruct((4, D), F32)...  162 us

profile of v4, /device:TPU:1, one launch (start us, length us, event | category | flops | bytes accessed | tf_op | source)
XLA Modules:
  0.0 172.9 jit_solution(3436835994872000039)
XLA Ops:
  0.6 0.0 copy-start
  0.6 0.0 copy-start.1
  0.7 1.4 reshape.31
  2.1 0.0 copy-done
  2.1 0.2 dynamic-slice_reduce_fusion
  2.3 0.7 reshape.27.block_ab_ref
  3.1 0.8 reshape.28.block_c_ref
  3.9 1.4 reshape.24
  5.3 0.3 copy.20
  5.5 0.9 reshape.25.q_ref
  6.4 0.0 copy-done.1
  6.4 1.5 reshape.26.own_ref
  7.9 161.8 %layer.1 = (f32[4,5120]{1,0:T(4,128)}, f32[4,5120]{1,0:T(4,128)}) custom-call(bf16[256,576]{1,0:T(8,128)(2,1)} %reshape.25.q_ref, bf16[512,576]{1,0:T(8,128)(2,1)} %reshape.26.own_ref, bf16[1,24,576]{2,1,0:T(8,128)(2,1)} %reshape.27.block_ab_ref, bf16[128,576]{1,0:T(8,128)(2,1)} %reshape.28.block_c_ref, s32[4,32]{1,0:T(4,128)} %list_ref.1, s32[4]{0:T(128)} %prefix_ref.1, ...), custom_call_target="tpu_custom_call" | custom-call | tf_op jit(solution)/shard_map/layer/pallas_call | solution.py:849
  169.8 1.5 copy.23
  171.3 1.5 copy.24
  (1 shorter events, 0.0 us)
Async XLA Ops:
  0.6 1.5 copy-start
  0.6 5.8 %copy-start.1 = (bf16[4,73728]{1,0:T(4,128)(2,1)S(1)}, bf16[4,73728]{1,0:T(4,128)(2,1)}, u32[]{:S(2)}) copy-start(bf16[4,73728]{1,0:T(4,128)(2,1)} %param.18) | copy-start | bytes 1769476
